TPU v7x, 32 devices: a whole 2x2x4 slice. The times are simulated.
32 devices in a mesh: row: 8 (over z, y), col: 4 (over x, core).
Axes of the slice: x: 2, y: 2, z: 4, core: 2. Of those that a mesh axis runs over, the one named last changes fastest.
Arguments:
- leaf_inverse: bfloat16 [32, 1024, 1024], P(('row', 'col')), as said below
- leaf_rhs: bfloat16 [32, 1024, 512], P(('row', 'col')), may hold values from -6 to 6
- leaf_tiles: bfloat16 [32, 1024, 1024], P(('row', 'col')), may hold values from -0.09375 to 0.09375
- mid_inverse_t: bfloat16 [8, 1024, 1024], P('col', None, 'row'), as said below
- mid_rhs: bfloat16 [8, 1024, 512], P('col', 'row'), may hold values from -6 to 6
- mid_tiles: bfloat16 [8, 1024, 1024], P('col', None, 'row'), may hold values from -0.125 to 0.125
- top_inverse_t: bfloat16 [2, 1024, 1024], P(None, None, 'col'), as said below
- top_rhs: bfloat16 [2, 1024, 512], P(None, 'col'), may hold values from -6 to 6
- tile_lists: int32 [32, 1], P(('row', 'col')), may hold values from 0 to 1
Outputs:
- leaf_solved: bfloat16 [32, 1024, 512], P(('row', 'col'))
- mid_solved: bfloat16 [8, 1024, 512], P('col', 'row')
- top_solved: bfloat16 [2, 1024, 512], P(None, 'col')
Inputs may be any that keep to these rules, and one draw needn't show every extreme that they name: Each leaf_inverse[d] is zero above its diagonal and has diagonal entries between 0.75 and 1.25. Each mid_inverse_t[q] is zero below its diagonal and has diagonal entries between 0.75 and 1.25. Each top_inverse_t[b] is zero below its diagonal and has diagonal entries between 0.75 and 1.25.
All inputs are finite; a program needn't handle non-finite values.
Results may differ from a plain program's by a relative error of at most 0.0065.
Values may be sent and summed in bfloat16 or wider, within the bound.
No kernel may reach another device: no remote copies, remote signals or barrier semaphores. Data moves between devices by JAX's collectives and lax.ppermute only.
A program may use at most 64 MiB of HBM per device.

v0:
```python
import jax
import jax.numpy as jnp
from jax import lax
from jax.experimental import pallas as pl
from jax.experimental.pallas import tpu as pltpu
from jax.sharding import PartitionSpec as P


CORES = 2
MARK = 16
LANES = 128


F32, BF16 = jnp.float32, jnp.bfloat16
VMEM = pl.BlockSpec(memory_space=pltpu.VMEM)
SMEM = pl.BlockSpec(memory_space=pltpu.SMEM)
HBM = pl.BlockSpec(memory_space=pltpu.HBM)


def wide(x):
    return x.astype(F32)


def total(terms):
    acc = terms[0]
    for term in terms[1:]:
        acc = acc + term
    return acc


def dot(a, b, a_dim):
    return lax.dot_general(a, b, (((a_dim,), (0,)), ((), ())), preferred_element_type=F32)


def in_hbm(x):
    return pltpu.with_memory_space_constraint(x, pltpu.HBM)


def call(body, shapes, args, specs=None, scratch=(), out_specs=None):
    return pl.pallas_call(
        body,
        out_shape=[jax.ShapeDtypeStruct(s, BF16) for s in shapes],
        in_specs=specs or [VMEM] * len(args),
        out_specs=out_specs or [VMEM] * len(shapes),
        scratch_shapes=scratch,
        compiler_params=pltpu.CompilerParams(vmem_limit_bytes=16 << 20),
    )(*args)


def fetch(source, target, sem):
    copy = pltpu.make_async_copy(source, target, sem)
    copy.start()
    return copy


def write_blocks(blocks, update, slot, rows, flip):
    chunks = update.shape[1] // LANES
    mark = jnp.full((MARK, LANES), slot[0, 0].astype(F32), F32).astype(BF16)
    for k, block in enumerate(blocks):
        at = pl.ds(pl.multiple_of((flip ^ k) * rows, rows), rows)
        for j in range(chunks):
            lanes = slice(j * LANES, (j + 1) * LANES)
            block[j * rows : (j + 1) * rows, :] = update[at, lanes]
        block[chunks * rows :, :] = mark


def leaf_stage(leaf_inverse, leaf_rhs, leaf_tiles, tile_lists, n_row):
    depth, src = leaf_rhs.shape
    half = n_row // 2
    rows = depth // n_row
    step = min(256, depth // 2)
    count = depth // step

    def body(inverse_hbm, rhs_hbm, tiles_hbm, slot, solved_hbm, solved, *rest):
        blocks = rest[:half]
        inverse, rhs, tiles, update, sems = rest[half:]
        row = lax.axis_index("row")
        base = (1 - row // half) * (depth // 2)
        spans = [slice(i * step, (i + 1) * step) for i in range(count)]
        first, second, stored = [], [], []
        for i, span in enumerate(spans):
            left = slice(0, (i + 1) * step)
            first.append(fetch(rhs_hbm.at[span], rhs.at[span], sems.at[0, i]))
            first.append(
                fetch(inverse_hbm.at[span, left], inverse.at[span, left], sems.at[1, i])
            )
        for i in range(count // 2):
            at = pl.ds(pl.multiple_of(base + i * step, step), step)
            second.append(fetch(tiles_hbm.at[at], tiles.at[spans[i]], sems.at[2, i]))
        for i, span in enumerate(spans):
            first[2 * i].wait()
            first[2 * i + 1].wait()
            block = dot(inverse[span, : (i + 1) * step], rhs[: (i + 1) * step, :], 1)
            solved[span, :] = block.astype(BF16)
            stored.append(fetch(solved.at[span], solved_hbm.at[span], sems.at[3, i]))
        for i in range(count // 2):
            second[i].wait()
            update[spans[i], :] = dot(tiles[spans[i], :], solved[...], 1).astype(BF16)
        write_blocks(blocks, update, slot, rows, row % half)
        for copy in stored:
            copy.wait()

    out = call(
        body,
        [(depth, src)] * 2 + [(src // LANES * rows + MARK, LANES)] * half,
        (*map(in_hbm, (leaf_inverse, leaf_rhs, leaf_tiles)), tile_lists),
        [HBM, HBM, HBM, SMEM],
        [
            pltpu.VMEM((depth, depth), BF16),
            pltpu.VMEM((depth, src), BF16),
            pltpu.VMEM((depth // 2, depth), BF16),
            pltpu.VMEM((depth // 2, src), BF16),
            pltpu.SemaphoreType.DMA((4, count)),
        ],
        [HBM] + [VMEM] * (half + 1),
    )
    return out[0], out[1], out[2:]


def near_stage(solved, leaf_tiles, tile_lists, mid_inverse_t, mid_tiles, n_row):
    depth, src = solved.shape
    nb, _, own_rows = mid_inverse_t.shape
    half = n_row // 2
    rows = depth // n_row

    def body(solved, tiles_hbm, slot, mid_inverse, mid_tile, swap, *rest):
        blocks, (tiles, update, sems) = rest[:half], rest[half:]
        row = lax.axis_index("row")
        at = pl.ds(pl.multiple_of(row // half * (depth // 2), depth // 2), depth // 2)
        copies = [
            fetch(tiles_hbm.at[at], tiles, sems.at[0]),
            fetch(mid_inverse.at[1 - row % nb], swap.at[0], sems.at[1]),
            fetch(mid_tile.at[1 - row % nb], swap.at[1], sems.at[2]),
        ]
        copies[0].wait()
        update[...] = dot(tiles[...], solved[...], 1).astype(BF16)
        write_blocks(blocks, update, slot, rows, row % half)
        for copy in copies[1:]:
            copy.wait()

    out = call(
        body,
        [(2, depth, own_rows)] + [(src // LANES * rows + MARK, LANES)] * half,
        (solved, in_hbm(leaf_tiles), tile_lists, *map(in_hbm, (mid_inverse_t, mid_tiles))),
        [VMEM, HBM, SMEM, HBM, HBM],
        [
            pltpu.VMEM((depth // 2, depth), BF16),
            pltpu.VMEM((depth // 2, src), BF16),
            pltpu.SemaphoreType.DMA((3,)),
        ],
    )
    return out[0], out[1:]


def slot_sums(blocks, nb, rows, chunk):
    sums = [None] * nb
    for ref in blocks:
        value = wide(ref[chunk * rows : (chunk + 1) * rows, :])
        mark = wide(ref[ref.shape[0] - MARK : ref.shape[0] - MARK + 1, :])
        for s in range(nb):
            term = jnp.where(mark == float(s), value, 0.0)
            sums[s] = term if sums[s] is None else sums[s] + term
    return sums


def by_block(sums, y):
    first, second = sums
    return jnp.where(y == 0, first, second), jnp.where(y == 0, second, first)


def cross_stage(blocks, nb, rows, src):
    def body(*refs):
        mine, other = refs[len(blocks) :]
        y = lax.axis_index("row") % nb
        for j in range(src // LANES):
            lanes = slice(j * LANES, (j + 1) * LANES)
            sums = by_block(slot_sums(refs[: len(blocks)], nb, rows, j), y)
            mine[:, lanes], other[:, lanes] = [value.astype(BF16) for value in sums]

    return call(body, [(rows, src)] * nb, tuple(blocks))


def near_sum_stage(blocks, mid_rhs):
    nb, rows, src = mid_rhs.shape

    def body(*refs):
        near, (rhs, mine, other) = refs[: len(blocks)], refs[len(blocks) :]
        y = lax.axis_index("row") % nb
        for j in range(src // LANES):
            lanes = slice(j * LANES, (j + 1) * LANES)
            sums = slot_sums(near, nb, rows, j)
            terms = by_block([wide(rhs[s, :, lanes]) - sums[s] for s in range(nb)], y)
            mine[:, lanes] = terms[0]
            other[:, lanes] = terms[1].astype(BF16)

    return pl.pallas_call(
        body,
        name="near_sum",
        out_shape=[
            jax.ShapeDtypeStruct((rows, src), F32),
            jax.ShapeDtypeStruct((rows, src), BF16),
        ],
        in_specs=[VMEM] * (len(blocks) + 1),
        out_specs=[VMEM] * 2,
        compiler_params=pltpu.CompilerParams(vmem_limit_bytes=16 << 20),
    )(*blocks, mid_rhs)


def resid_stage(*pairs):
    count = len(pairs)

    def body(*refs):
        for near, far, out in zip(refs[:count], refs[count : 2 * count], refs[2 * count :]):
            out[...] = (wide(near[...]) - wide(far[...])).astype(BF16)

    args = [near for near, _ in pairs] + [far for _, far in pairs]
    return call(body, [pairs[0][1].shape] * count, tuple(args))


def early_stage(blocks, owners, mid_inverse_t, swapped):
    nb, _, rows = mid_inverse_t.shape
    src = blocks[0].shape[1]

    def body(*refs):
        parts, (inverse, swap, out) = refs[: len(blocks)], refs[len(blocks) :]
        out[...] = solve_share(parts, owners, inverse, swap, nb, rows)

    return pl.pallas_call(
        body,
        name="early",
        out_shape=jax.ShapeDtypeStruct((2 * rows, src), F32),
        in_specs=[VMEM] * (len(blocks) + 2),
        out_specs=VMEM,
        compiler_params=pltpu.CompilerParams(vmem_limit_bytes=16 << 20),
    )(*blocks, mid_inverse_t, swapped)


def solve_share(parts, owners, inverse, swap, nb, rows):
    row = lax.axis_index("row")
    z, y = row // nb, row % nb
    acc = None
    for owner, ref in zip(owners, parts):
        at = pl.ds(pl.multiple_of(owner(z, y) * rows, rows), rows)
        part = jnp.concatenate([inverse[y, at, :], swap[0, at, :]], axis=1)
        term = dot(part, ref[...], 0)
        acc = term if acc is None else acc + term
    return acc


def mid_stage(blocks, owners, early, mid_inverse_t, mid_tiles, swapped, n_x, own_top):
    nb, _, rows = mid_inverse_t.shape
    src = blocks[0].shape[1]
    count = len(blocks)

    def body(*refs):
        parts, (start, inverse, tiles, swap, own, other, sent) = refs[:count], refs[count:]
        core = lax.axis_index("col") % CORES
        y = lax.axis_index("row") % nb
        acc = start[...] + solve_share(parts, owners, inverse, swap, nb, rows)
        solved = acc.astype(BF16)
        own[...] = solved[:rows]
        other[...] = solved[rows:]
        for x in range(n_x):
            at = pl.ds(pl.multiple_of((x * CORES + 1 - core) * own_top, own_top), own_top)
            part = jnp.concatenate([tiles[y, at, :], swap[1, at, :]], axis=1)
            sent[x] = dot(part, solved, 1).astype(BF16)

    return call(
        body,
        [(rows, src), (rows, src), (n_x, own_top, src)],
        (*blocks, early, mid_inverse_t, mid_tiles, swapped),
    )


def core_stage(own, other, mid_tiles, swapped, got, n_z):
    n_x, own_top, src = got.shape
    nb = mid_tiles.shape[0]
    width = src // n_z
    dense = width % LANES == 0

    def body(own, other, tiles, swap, far, *rest):
        outs, part = (rest[:-1], rest[-1]) if dense else (None, rest[0])
        row, core = lax.axis_index("row"), lax.axis_index("col") % CORES
        z, y = row // nb, row % nb
        solved = jnp.concatenate([own[...], other[...]], axis=0)
        for x in range(n_x):
            at = pl.ds(pl.multiple_of((x * CORES + core) * own_top, own_top), own_top)
            tile = jnp.concatenate([tiles[y, at, :], swap[1, at, :]], axis=1)
            term = dot(tile, solved, 1) + wide(far[x])
            part[x * own_top : (x + 1) * own_top, :] = term.astype(BF16)
        for k in range(n_z if dense else 0):
            lanes = pl.ds(pl.multiple_of((z ^ k) * width, width), width)
            outs[k][...] = part[:, lanes]

    args = (own, other, mid_tiles, swapped, got)
    rows = n_x * own_top
    if dense:
        return call(body, [(rows, width)] * n_z, args, scratch=[pltpu.VMEM((rows, src), BF16)])
    part = call(body, [(rows, src)], args)[0]
    z = lax.axis_index("row") // nb
    return [lax.dynamic_slice_in_dim(part, (z ^ k) * width, width, 1) for k in range(n_z)]


def share_stage(top_rhs, n_z):
    n_top, rows, src = top_rhs.shape
    width = src // n_z
    row = lax.axis_index("row")
    if width % LANES:
        part = lax.dynamic_index_in_dim(top_rhs, row % n_top, 0, keepdims=False)
        return lax.dynamic_slice_in_dim(part, row // n_top * width, width, 1)

    def body(rhs, out):
        row = lax.axis_index("row")
        lanes = pl.ds(pl.multiple_of(row // n_top * width, width), width)
        out[...] = rhs[row % n_top, :, lanes]

    return call(body, [(rows, width)], (top_rhs,))[0]


def sum_stage(pieces):
    def body(*refs):
        refs[-1][...] = total([wide(ref[...]) for ref in refs[:-1]]).astype(BF16)

    return call(body, [pieces[0].shape], tuple(pieces))[0]


def top_resid_stage(pieces, shares):
    n_x = len(shares)
    rows, width = shares[0].shape

    def body(*refs):
        terms, rhs, out = refs[: len(pieces)], refs[len(pieces) : -1], refs[-1]
        x = lax.axis_index("col") // CORES
        for dx in range(n_x):
            at = pl.ds(pl.multiple_of((x ^ dx) * rows, rows), rows)
            update = total([wide(ref[at, :]) for ref in terms])
            out[at, :] = (wide(rhs[dx][...]) - update).astype(BF16)

    return call(body, [(n_x * rows, width)], (*pieces, *shares))[0]


def top_solve_stage(pieces, top_inverse_t):
    n_top, _, rows = top_inverse_t.shape
    width = pieces[0].shape[1]
    n_x = pieces[0].shape[0] // rows

    def body(*refs):
        parts, inverse, out = refs[:CORES], refs[CORES], refs[CORES + 1]
        y, core = lax.axis_index("row") % n_top, lax.axis_index("col") % CORES
        acc = None
        for k, ref in enumerate(parts):
            for x in range(n_x):
                start = pl.multiple_of((x * CORES + (core ^ k)) * rows, rows)
                part = ref[x * rows : (x + 1) * rows, :]
                term = dot(inverse[y, pl.ds(start, rows), :], part, 0)
                acc = term if acc is None else acc + term
        out[...] = acc.astype(BF16)

    return call(body, [(rows, width)], (*pieces, top_inverse_t))[0]


def spread_stage(pieces, n_z, n_top):
    rows, width = pieces[0].shape
    count = len(pieces)

    def body(*refs):
        out, sems = refs[count:]
        row = lax.axis_index("row")
        copies = []
        for k, ref in enumerate(refs[:count]):
            z, y = (row ^ k) // n_top, (row ^ k) % n_top
            lanes = pl.ds(pl.multiple_of(z * width, width), width)
            copies.append(fetch(ref, out.at[y, :, lanes], sems.at[k]))
        for copy in copies:
            copy.wait()

    return call(
        body,
        [(n_top, rows, n_z * width)],
        tuple(pieces),
        scratch=[pltpu.SemaphoreType.DMA((count,))],
        out_specs=[HBM],
    )[0]


def narrow_spread(pieces, n_z, n_top):
    rows, width = pieces[0].shape
    row = lax.axis_index("row")
    out = jnp.zeros((n_z * n_top, rows, width), BF16)
    for k, piece in enumerate(pieces):
        out = lax.dynamic_update_index_in_dim(out, piece, row ^ k, 0)
    out = out.reshape(n_z, n_top, rows, width).transpose(1, 2, 0, 3)
    return out.reshape(n_top, rows, n_z * width)


def make_local(n_row, n_col):
    n_x = n_col // CORES
    half = n_row // 2

    def row_xor(x, k):
        return lax.ppermute(x, "row", [(i, i ^ k) for i in range(n_row)])

    def col_xor(x, k):
        return lax.ppermute(x, "col", [(i, i ^ k) for i in range(n_col)])

    def local(
        leaf_inverse,
        leaf_rhs,
        leaf_tiles,
        mid_inverse_t,
        mid_rhs,
        mid_tiles,
        top_inverse_t,
        top_rhs,
        tile_lists,
    ):
        nb, _, own_rows = mid_inverse_t.shape
        n_top, _, own_top = top_inverse_t.shape
        src = leaf_rhs.shape[2]
        n_z = n_row // n_top

        solved_leaf, solved, far = leaf_stage(
            leaf_inverse[0], leaf_rhs[0], leaf_tiles[0], tile_lists, n_row
        )
        swap, near = near_stage(
            solved, leaf_tiles[0], tile_lists, mid_inverse_t, mid_tiles, n_row
        )

        crossing, staying = [far[0]], [near[0]]
        for k in range(1, half):
            crossing.append(row_xor(far[k], k))
        for k in range(1, half):
            staying.append(row_xor(near[k], k))
        mine, other = cross_stage(crossing, nb, own_rows, src)
        far_mine = row_xor(mine, half)
        far_given = row_xor(other, half ^ 1)
        near_mine, other = near_sum_stage(staying, mid_rhs)

        y = lax.axis_index("row") % nb
        swapped = row_xor(swap, 1)
        share = share_stage(top_rhs, n_z)
        shares = [share] + [col_xor(share, dx * CORES) for dx in range(1, n_x)]

        def move(block, *hops):
            pairs = [(f * nb + j, t * nb + j) for f, t in hops for j in range(nb)]
            return lax.ppermute(block, "row", pairs)

        near_given = row_xor(other, 1)
        start = resid_stage((near_mine, far_mine), (near_given, far_given))
        blocks, owners = [start], [lambda z: z]
        if n_z == 4:
            z = lax.axis_index("row") // nb
            first, second, third = [], [], []
            for part, b in zip("ab", start):
                first.append(move(b, (0, 2), (2, 3)))
                second.append(move(b, (0, 1), (1, 3)))
            for part, b, f in zip("ab", start, first):
                passed = jnp.where(z == 2, f, b)
                third.append(move(passed, (1, 2), (2, 3)))
            blocks += [first, second, third]
            owners += [
                lambda z: jnp.where(z == 3, 2, 0),
                lambda z: jnp.where(z == 3, 1, 0),
                lambda z: jnp.where(z == 2, 1, 0),
            ]
        else:
            for away in range(1, n_z):
                by = 2 - away % 2
                hops = [(f, f + by) for f in range(away - by, n_z - by)]
                moved = []
                for part, b in zip("ab", blocks[away - by]):
                    moved.append(move(b, *hops))
                blocks.append(moved)
                owners.append(lambda z, away=away: (z - away + n_z) % n_z)
        flat = [b for pair in blocks for b in pair]
        by_row = [
            lambda z, y, owner=owner, k=k: owner(z) * nb + (y ^ k)
            for owner in owners
            for k in range(2)
        ]
        late = [6, 7] if n_z == 4 else [len(flat) - 2, len(flat) - 1]
        soon = [i for i in range(len(flat)) if i not in late]
        early = early_stage(
            [flat[i] for i in soon], [by_row[i] for i in soon], mid_inverse_t, swapped
        )
        own, other, sent = mid_stage(
            [flat[i] for i in late],
            [by_row[i] for i in late],
            early,
            mid_inverse_t,
            mid_tiles,
            swapped,
            n_x,
            own_top,
        )
        sent = col_xor(sent, 1)
        other_own = row_xor(other, 1)
        mid_own = jnp.where(
            y == 0, jnp.stack([own, other_own]), jnp.stack([other_own, own])
        )

        pieces = list(core_stage(own, other, mid_tiles, swapped, sent, n_z))
        for k in range(1, n_z):
            pieces[k] = row_xor(pieces[k], k * n_top)
        part = sum_stage(pieces)
        parts = [part] + [col_xor(part, dx * CORES) for dx in range(1, n_x)]
        own = top_resid_stage(parts, shares)

        mine = top_solve_stage([own, col_xor(own, 1)], top_inverse_t)
        got = [mine]
        for k in range(1, n_z):
            got.append(row_xor(mine, k * n_top))
        spread_to = []
        for piece in got:
            spread_to += [row_xor(piece, k) if k else piece for k in range(n_top)]
        got = spread_to
        spread = narrow_spread if mine.shape[1] % LANES else spread_stage
        top_own = spread(got, n_z, n_top)
        return solved_leaf[None], mid_own, top_own

    return local


def solution(mesh):
    placed = (
        P(("row", "col"), None, None),
        P(("row", "col"), None, None),
        P(("row", "col"), None, None),
        P("col", None, "row"),
        P("col", "row", None),
        P("col", None, "row"),
        P(None, None, "col"),
        P(None, "col", None),
        P(("row", "col"), None),
    )
    return jax.shard_map(
        make_local(mesh.shape["row"], mesh.shape["col"]),
        mesh=mesh,
        in_specs=placed,
        out_specs=(P(("row", "col"), None, None), P("col", "row", None), P(None, "col", None)),
        check_vma=False,
    )
```

profile of v0, /device:TPU:0, one launch (start us, length us, event | category | flops | bytes accessed | tf_op | source)
XLA Modules:
  0.0 95.9 jit_solution(1667888258002249607)
XLA Ops:
  1.3 3.4 %shard_map.112 = (bf16[1024,512]{1,0:T(8,128)(2,1)}, bf16[1024,512]{1,0:T(8,128)(2,1)S(1)}, bf16[528,128]{1,0:T(8,128)(2,1)S(1)}, bf16[528,128]{1,0:T(8,128)(2,1...) custom-call(bf16[1024,1024]{1,0:T(8,128)(2,1)} %bitcast.9, bf16[1024,512]{1,0:T(8,128)(2,1)} %bitcast.10, ...), custom_call_target="tpu_custom_call" | custom-call | tf_op jit(solution)/shard_map/pallas_call | solution.py:40
  4.7 3.1 %collective-permute-start.4 = (bf16[528,128]{1,0:T(8,128)(2,1)S(1)}, bf16[528,128]{1,0:T(8,128)(2,1)S(1)}, u32[]{:S(2)}, u32[]{:S(2)}) collective-permute-start(bf16[528,128]{1,0:T(8,128)(2,1)S(1)} %get-tuple-element.36), channel_id=1, source_target_pairs={{0,4},{4,0},{8,12},{12,8},{16,20},{20,16},{24,28},{28,24},{1,5},{5... | collective-permute-start | bytes 405512 | tf_op jit(solution)/shard_map/ppermute | solution.py:401
  7.8 1.6 %collective-permute-start.5 = (bf16[528,128]{1,0:T(8,128)(2,1)S(1)}, bf16[528,128]{1,0:T(8,128)(2,1)S(1)}, u32[]{:S(2)}, u32[]{:S(2)}) collective-permute-start(bf16[528,128]{1,0:T(8,128)(2,1)S(1)} %get-tuple-element.37), channel_id=1, source_target_pairs={{0,8},{4,12},{8,0},{12,4},{16,24},{20,28},{24,16},{28,20},{1,9},{5... | collective-permute-start | bytes 405512 | tf_op jit(solution)/shard_map/ppermute | solution.py:401
  9.4 0.0 collective-permute-start.6
  9.4 2.1 %shard_map.113 = (bf16[2,1024,128]{2,1,0:T(8,128)(2,1)S(1)}, bf16[528,128]{1,0:T(8,128)(2,1)S(1)}, bf16[528,128]{1,0:T(8,128)(2,1)S(1)}, bf16[528,128]{1,0:T(8,128)(2,1)S(1)}, bf16[528,128]{1,0:T(8,128)(2,1)S(1)}) custom-call(bf16[1024,512]{1,0:T(8,128)(2,1)S(1)} %get-tuple-element.28.solved, bf16[1024,1024]{1,0:T(8,128)(2,1)} %bitcast.8, ...), custom_call_target="tpu_custom_call" | custom-call | tf_op jit(solution)/shard_map/pallas_call | solution.py:40
  11.5 0.0 copy-start.1
  11.5 2.0 %collective-permute-start = (bf16[528,128]{1,0:T(8,128)(2,1)S(1)}, bf16[528,128]{1,0:T(8,128)(2,1)S(1)}, u32[]{:S(2)}, u32[]{:S(2)}) collective-permute-start(bf16[528,128]{1,0:T(8,128)(2,1)S(1)} %get-tuple-element.30), channel_id=1, source_target_pairs={{0,4},{4,0},{8,12},{12,8},{16,20},{20,16},{24,28},{28,24},{1,5},{5... | collective-permute-start | bytes 405512 | tf_op jit(solution)/shard_map/ppermute | solution.py:401
  13.5 1.6 %collective-permute-start.1 = (bf16[528,128]{1,0:T(8,128)(2,1)S(1)}, bf16[528,128]{1,0:T(8,128)(2,1)S(1)}, u32[]{:S(2)}, u32[]{:S(2)}) collective-permute-start(bf16[528,128]{1,0:T(8,128)(2,1)S(1)} %get-tuple-element.31), channel_id=1, source_target_pairs={{0,8},{4,12},{8,0},{12,4},{16,24},{20,28},{24,16},{28,20},{1,9},{5... | collective-permute-start | bytes 405512 | tf_op jit(solution)/shard_map/ppermute | solution.py:401
  15.0 0.0 collective-permute-start.2
  15.0 1.4 %collective-permute-done.6.refs_3_ = bf16[528,128]{1,0:T(8,128)(2,1)S(1)} collective-permute-done((bf16[528,128]{1,0:T(8,128)(2,1)S(1)}, bf16[528,128]{1,0:T(8,128)(2,1)S(1)}, u32[]{:S(2)}, u32[]{:S(2)}) %collective-permute-start.6) | collective-permute-done | bytes 135200 | tf_op jit(solution)/shard_map/ppermute | solution.py:401
  16.4 0.2 shard_map.114
  16.6 2.9 %collective-permute-start.7 = (bf16[128,512]{1,0:T(8,128)(2,1)S(1)}, bf16[128,512]{1,0:T(8,128)(2,1)S(1)}, u32[]{:S(2)}, u32[]{:S(2)}) collective-permute-start(bf16[128,512]{1,0:T(8,128)(2,1)S(1)} %get-tuple-element.39), channel_id=1, source_target_pairs={{0,16},{4,20},{8,24},{12,28},{16,0},{20,4},{24,8},{28,12},{1,17},{... | collective-permute-start | bytes 393224 | tf_op jit(solution)/shard_map/ppermute | solution.py:401
  19.5 1.3 %collective-permute-start.8 = (bf16[128,512]{1,0:T(8,128)(2,1)S(1)}, bf16[128,512]{1,0:T(8,128)(2,1)S(1)}, u32[]{:S(2)}, u32[]{:S(2)}) collective-permute-start(bf16[128,512]{1,0:T(8,128)(2,1)S(1)} %get-tuple-element.40), channel_id=1, source_target_pairs={{0,20},{4,16},{8,28},{12,24},{16,4},{20,0},{24,12},{28,8},{1,21},{... | collective-permute-start | bytes 393224 | tf_op jit(solution)/shard_map/ppermute | solution.py:401
  20.8 1.7 %collective-permute-done.1.refs_2_ = bf16[528,128]{1,0:T(8,128)(2,1)S(1)} collective-permute-done((bf16[528,128]{1,0:T(8,128)(2,1)S(1)}, bf16[528,128]{1,0:T(8,128)(2,1)S(1)}, u32[]{:S(2)}, u32[]{:S(2)}) %collective-permute-start.1) | collective-permute-done | bytes 135200 | tf_op jit(solution)/shard_map/ppermute | solution.py:401
  22.5 1.7 %collective-permute-done.2.refs_3_ = bf16[528,128]{1,0:T(8,128)(2,1)S(1)} collective-permute-done((bf16[528,128]{1,0:T(8,128)(2,1)S(1)}, bf16[528,128]{1,0:T(8,128)(2,1)S(1)}, u32[]{:S(2)}, u32[]{:S(2)}) %collective-permute-start.2) | collective-permute-done | bytes 135200 | tf_op jit(solution)/shard_map/ppermute | solution.py:401
  24.2 0.2 near_sum.1
  24.5 0.0 copy-start
  24.5 2.7 %collective-permute-start.3 = (bf16[128,512]{1,0:T(8,128)(2,1)S(1)}, bf16[128,512]{1,0:T(8,128)(2,1)S(1)}, u32[]{:S(2)}, u32[]{:S(2)}) collective-permute-start(bf16[128,512]{1,0:T(8,128)(2,1)S(1)} %get-tuple-element.34), channel_id=1, source_target_pairs={{0,4},{4,0},{8,12},{12,8},{16,20},{20,16},{24,28},{28,24},{1,5},{5... | collective-permute-start | bytes 393224 | tf_op jit(solution)/shard_map/ppermute | solution.py:401
  27.1 2.3 %collective-permute-done.7.refs_2_ = bf16[128,512]{1,0:T(8,128)(2,1)S(1)} collective-permute-done((bf16[128,512]{1,0:T(8,128)(2,1)S(1)}, bf16[128,512]{1,0:T(8,128)(2,1)S(1)}, u32[]{:S(2)}, u32[]{:S(2)}) %collective-permute-start.7) | collective-permute-done | bytes 131104 | tf_op jit(solution)/shard_map/ppermute | solution.py:401
  29.4 2.2 %collective-permute-done.8.refs_3_ = bf16[128,512]{1,0:T(8,128)(2,1)S(1)} collective-permute-done((bf16[128,512]{1,0:T(8,128)(2,1)S(1)}, bf16[128,512]{1,0:T(8,128)(2,1)S(1)}, u32[]{:S(2)}, u32[]{:S(2)}) %collective-permute-start.8) | collective-permute-done | bytes 131104 | tf_op jit(solution)/shard_map/ppermute | solution.py:401
  31.7 0.0 collective-permute-done.3.refs_1_
  31.7 0.1 shard_map.115
  31.7 2.6 %collective-permute-start.9 = (bf16[128,512]{1,0:T(8,128)(2,1)S(1)}, bf16[128,512]{1,0:T(8,128)(2,1)S(1)}, u32[]{:S(2)}, u32[]{:S(2)}) collective-permute-start(bf16[128,512]{1,0:T(8,128)(2,1)S(1)} %get-tuple-element.41.refs_0_), channel_id=1, source_target_pairs={{0,16},{4,20},{16,24},{20,28},{1,17},{5,21},{17,25},{21,29},{2,18}... | collective-permute-start | bytes 393224 | tf_op jit(solution)/shard_map/ppermute | solution.py:446
  34.4 1.0 %collective-permute-start.15 = (bf16[2,1024,128]{2,1,0:T(8,128)(2,1)S(1)}, bf16[2,1024,128]{2,1,0:T(8,128)(2,1)S(1)}, u32[]{:S(2)}, u32[]{:S(2)}) collective-permute-start(bf16[2,1024,128]{2,1,0:T(8,128)(2,1)S(1)} %get-tuple-element.43), channel_id=1, source_target_pairs={{0,4},{4,0},{8,12},{12,8},{16,20},{20,16},{24,28},{28,24},{1,5},{5... | collective-permute-start | bytes 1572872 | tf_op jit(solution)/shard_map/ppermute | solution.py:401
  35.4 1.3 %collective-permute-start.13 = (bf16[128,512]{1,0:T(8,128)(2,1)S(1)}, bf16[128,512]{1,0:T(8,128)(2,1)S(1)}, u32[]{:S(2)}, u32[]{:S(2)}) collective-permute-start(bf16[128,512]{1,0:T(8,128)(2,1)S(1)} %get-tuple-element.41.refs_0_), channel_id=1, source_target_pairs={{0,8},{4,12},{8,24},{12,28},{1,9},{5,13},{9,25},{13,29},{2,10},{6,... | collective-permute-start | bytes 393224 | tf_op jit(solution)/shard_map/ppermute | solution.py:446
  36.6 5.1 %collective-permute-start.14 = (bf16[128,512]{1,0:T(8,128)(2,1)S(1)}, bf16[128,512]{1,0:T(8,128)(2,1)S(1)}, u32[]{:S(2)}, u32[]{:S(2)}) collective-permute-start(bf16[128,512]{1,0:T(8,128)(2,1)S(1)} %get-tuple-element.42.refs_1_), channel_id=1, source_target_pairs={{0,8},{4,12},{8,24},{12,28},{1,9},{5,13},{9,25},{13,29},{2,10},{6,... | collective-permute-start | bytes 393224 | tf_op jit(solution)/shard_map/ppermute | solution.py:446
  41.7 1.3 %collective-permute-start.11 = (bf16[128,512]{1,0:T(8,128)(2,1)S(1)}, bf16[128,512]{1,0:T(8,128)(2,1)S(1)}, u32[]{:S(2)}, u32[]{:S(2)}) collective-permute-start(bf16[128,512]{1,0:T(8,128)(2,1)S(1)} %get-tuple-element.42.refs_1_), channel_id=1, source_target_pairs={{0,16},{4,20},{16,24},{20,28},{1,17},{5,21},{17,25},{21,29},{2,18}... | collective-permute-start | bytes 393224 | tf_op jit(solution)/shard_map/ppermute | solution.py:446
  43.0 0.7 collective-permute-start.10
  43.7 1.9 %collective-permute-done.11.refs_3_ = bf16[128,512]{1,0:T(8,128)(2,1)S(1)} collective-permute-done((bf16[128,512]{1,0:T(8,128)(2,1)S(1)}, bf16[128,512]{1,0:T(8,128)(2,1)S(1)}, u32[]{:S(2)}, u32[]{:S(2)}) %collective-permute-start.11) | collective-permute-done | bytes 131104 | tf_op jit(solution)/shard_map/ppermute | solution.py:446
  45.6 0.7 collective-permute-start.12
  46.3 1.1 %collective-permute-done.15.refs_7_.refs_5_.swap = bf16[2,1024,128]{2,1,0:T(8,128)(2,1)S(1)} collective-permute-done((bf16[2,1024,128]{2,1,0:T(8,128)(2,1)S(1)}, bf16[2,1024,128]{2,1,0:T(8,128)(2,1)S(1)}, u32[]{:S(2)}, u32[]{:S(2)}) %collective-permute-start.15) | collective-permute-done | bytes 524320 | tf_op jit(solution)/shard_map/ppermute | solution.py:401
  47.4 0.6 early.1.refs_2_
  48.0 0.0 copy-start.3
  48.1 0.6 shard_map.116
  48.7 0.0 copy-start.2
  48.7 0.1 collective-permute-start.17
  48.8 1.9 %collective-permute-done.17.far = bf16[2,256,512]{2,1,0:T(8,128)(2,1)S(1)} collective-permute-done((bf16[2,256,512]{2,1,0:T(8,128)(2,1)S(1)}, bf16[2,256,512]{2,1,0:T(8,128)(2,1)S(1)}, u32[]{:S(2)}, u32[]{:S(2)}) %collective-permute-start.17) | collective-permute-done | bytes 524320 | tf_op jit(solution)/shard_map/ppermute | solution.py:404
  50.7 0.4 shard_map.117
  51.1 6.0 %collective-permute-start.18 = (bf16[512,128]{1,0:T(8,128)(2,1)S(1)}, bf16[512,128]{1,0:T(8,128)(2,1)S(1)}, u32[]{:S(2)}, u32[]{:S(2)}) collective-permute-start(bf16[512,128]{1,0:T(8,128)(2,1)S(1)} %get-tuple-element.48), channel_id=1, source_target_pairs={{0,8},{4,12},{8,0},{12,4},{16,24},{20,28},{24,16},{28,20},{1,9},{5... | collective-permute-start | bytes 393224 | tf_op jit(solution)/shard_map/ppermute | solution.py:401
  57.1 3.1 %collective-permute-start.19 = (bf16[512,128]{1,0:T(8,128)(2,1)S(1)}, bf16[512,128]{1,0:T(8,128)(2,1)S(1)}, u32[]{:S(2)}, u32[]{:S(2)}) collective-permute-start(bf16[512,128]{1,0:T(8,128)(2,1)S(1)} %get-tuple-element.49), channel_id=1, source_target_pairs={{0,16},{4,20},{8,24},{12,28},{16,0},{20,4},{24,8},{28,12},{1,17},{... | collective-permute-start | bytes 393224 | tf_op jit(solution)/shard_map/ppermute | solution.py:401
  60.3 0.2 collective-permute-start.20
  60.5 0.5 collective-permute-done.18.refs_1_
  60.9 9.3 %collective-permute-done.19.refs_2_ = bf16[512,128]{1,0:T(8,128)(2,1)S(1)} collective-permute-done((bf16[512,128]{1,0:T(8,128)(2,1)S(1)}, bf16[512,128]{1,0:T(8,128)(2,1)S(1)}, u32[]{:S(2)}, u32[]{:S(2)}) %collective-permute-start.19) | collective-permute-done | bytes 131104 | tf_op jit(solution)/shard_map/ppermute | solution.py:401
  70.2 0.1 shard_map.118.refs_0_
  70.3 1.5 %collective-permute-start.21 = (bf16[512,128]{1,0:T(8,128)(2,1)S(1)}, bf16[512,128]{1,0:T(8,128)(2,1)S(1)}, u32[]{:S(2)}, u32[]{:S(2)}) collective-permute-start(bf16[512,128]{1,0:T(8,128)(2,1)S(1)} %shard_map.118.refs_0_), channel_id=1, source_target_pairs={{0,2},{1,3},{2,0},{3,1},{4,6},{5,7},{6,4},{7,5},{8,10},{9,11},{10,... | collective-permute-start | bytes 393224 | tf_op jit(solution)/shard_map/ppermute | solution.py:404
  71.9 0.6 collective-permute-start.22
  72.5 3.7 %collective-permute-done.22.refs_3_ = bf16[256,128]{1,0:T(8,128)(2,1)S(1)} collective-permute-done((bf16[256,128]{1,0:T(8,128)(2,1)S(1)}, bf16[256,128]{1,0:T(8,128)(2,1)S(1)}, u32[]{:S(2)}, u32[]{:S(2)}) %collective-permute-start.22) | collective-permute-done | bytes 65568 | tf_op jit(solution)/shard_map/ppermute | solution.py:404
  76.2 0.1 shard_map.120.refs_0_
  76.3 0.1 collective-permute-start.23
  76.3 2.4 %collective-permute-start.16 = (bf16[128,512]{1,0:T(8,128)(2,1)S(1)}, bf16[128,512]{1,0:T(8,128)(2,1)S(1)}, u32[]{:S(2)}, u32[]{:S(2)}) collective-permute-start(bf16[128,512]{1,0:T(8,128)(2,1)S(1)} %get-tuple-element.45.other), channel_id=1, source_target_pairs={{0,4},{4,0},{8,12},{12,8},{16,20},{20,16},{24,28},{28,24},{1,5},{5... | collective-permute-start | bytes 393224 | tf_op jit(solution)/shard_map/ppermute | solution.py:401
  78.7 0.4 shard_map.121.refs_0_
  79.1 2.6 %collective-permute-start.29 = (bf16[256,128]{1,0:T(8,128)(2,1)S(1)}, bf16[256,128]{1,0:T(8,128)(2,1)S(1)}, u32[]{:S(2)}, u32[]{:S(2)}) collective-permute-start(bf16[256,128]{1,0:T(8,128)(2,1)S(1)} %shard_map.121.refs_0_), channel_id=1, source_target_pairs={{0,24},{4,28},{8,16},{12,20},{16,8},{20,12},{24,0},{28,4},{1,25},{... | collective-permute-start | bytes 196616 | tf_op jit(solution)/shard_map/ppermute | solution.py:401
  81.7 1.8 %collective-permute-start.27 = (bf16[256,128]{1,0:T(8,128)(2,1)S(1)}, bf16[256,128]{1,0:T(8,128)(2,1)S(1)}, u32[]{:S(2)}, u32[]{:S(2)}) collective-permute-start(bf16[256,128]{1,0:T(8,128)(2,1)S(1)} %shard_map.121.refs_0_), channel_id=1, source_target_pairs={{0,16},{4,20},{8,24},{12,28},{16,0},{20,4},{24,8},{28,12},{1,17},{... | collective-permute-start | bytes 196616 | tf_op jit(solution)/shard_map/ppermute | solution.py:401
  83.5 0.1 collective-permute-start.25
  83.6 1.3 %collective-permute-start.24 = (bf16[256,128]{1,0:T(8,128)(2,1)S(1)}, bf16[256,128]{1,0:T(8,128)(2,1)S(1)}, u32[]{:S(2)}, u32[]{:S(2)}) collective-permute-start(bf16[256,128]{1,0:T(8,128)(2,1)S(1)} %shard_map.121.refs_0_), channel_id=1, source_target_pairs={{0,4},{4,0},{8,12},{12,8},{16,20},{20,16},{24,28},{28,24},{1,5},{5... | collective-permute-start | bytes 196616 | tf_op jit(solution)/shard_map/ppermute | solution.py:401
  84.8 0.4 collective-permute-done.29.refs_6_
  85.2 1.3 %collective-permute-start.30 = (bf16[256,128]{1,0:T(8,128)(2,1)S(1)}, bf16[256,128]{1,0:T(8,128)(2,1)S(1)}, u32[]{:S(2)}, u32[]{:S(2)}) collective-permute-start(bf16[256,128]{1,0:T(8,128)(2,1)S(1)} %collective-permute-done.29.refs_6_), channel_id=1, source_target_pairs={{0,4},{4,0},{8,12},{12,8},{16,20},{20,16},{24,28},{28,24},{1,5},{5... | collective-permute-start | bytes 196616 | tf_op jit(solution)/shard_map/ppermute | solution.py:401
  86.5 2.8 %collective-permute-done.27.refs_4_ = bf16[256,128]{1,0:T(8,128)(2,1)S(1)} collective-permute-done((bf16[256,128]{1,0:T(8,128)(2,1)S(1)}, bf16[256,128]{1,0:T(8,128)(2,1)S(1)}, u32[]{:S(2)}, u32[]{:S(2)}) %collective-permute-start.27) | collective-permute-done | bytes 65568 | tf_op jit(solution)/shard_map/ppermute | solution.py:401
  89.3 1.3 %collective-permute-start.28 = (bf16[256,128]{1,0:T(8,128)(2,1)S(1)}, bf16[256,128]{1,0:T(8,128)(2,1)S(1)}, u32[]{:S(2)}, u32[]{:S(2)}) collective-permute-start(bf16[256,128]{1,0:T(8,128)(2,1)S(1)} %collective-permute-done.27.refs_4_), channel_id=1, source_target_pairs={{0,4},{4,0},{8,12},{12,8},{16,20},{20,16},{24,28},{28,24},{1,5},{5... | collective-permute-start | bytes 196616 | tf_op jit(solution)/shard_map/ppermute | solution.py:401
  90.6 0.8 collective-permute-start.26
  91.4 0.7 maximum_select_fusion
  92.1 2.2 %collective-permute-done.28.refs_5_ = bf16[256,128]{1,0:T(8,128)(2,1)S(1)} collective-permute-done((bf16[256,128]{1,0:T(8,128)(2,1)S(1)}, bf16[256,128]{1,0:T(8,128)(2,1)S(1)}, u32[]{:S(2)}, u32[]{:S(2)}) %collective-permute-start.28) | collective-permute-done | bytes 65568 | tf_op jit(solution)/shard_map/ppermute | solution.py:401
  94.3 0.7 collective-permute-done.26.refs_3_
  95.0 0.8 shard_map.122
  (24 shorter events, 0.1 us)
Async XLA Ops:
  4.7 10.3 %collective-permute-start.4 = (bf16[528,128]{1,0:T(8,128)(2,1)S(1)}, bf16[528,128]{1,0:T(8,128)(2,1)S(1)}, u32[]{:S(2)}, u32[]{:S(2)}) collective-permute-start(bf16[528,128]{1,0:T(8,128)(2,1)S(1)} %get-tuple-element.36), channel_id=1, source_target_pairs={{0,4},{4,0},{8,12},{12,8},{16,20},{20,16},{24,28},{28,24},{1,5},{5... | collective-permute-start | bytes 405512 | tf_op jit(solution)/shard_map/ppermute | solution.py:401
  7.8 7.3 %collective-permute-start.5 = (bf16[528,128]{1,0:T(8,128)(2,1)S(1)}, bf16[528,128]{1,0:T(8,128)(2,1)S(1)}, u32[]{:S(2)}, u32[]{:S(2)}) collective-permute-start(bf16[528,128]{1,0:T(8,128)(2,1)S(1)} %get-tuple-element.37), channel_id=1, source_target_pairs={{0,8},{4,12},{8,0},{12,4},{16,24},{20,28},{24,16},{28,20},{1,9},{5... | collective-permute-start | bytes 405512 | tf_op jit(solution)/shard_map/ppermute | solution.py:401
  9.4 7.1 %collective-permute-start.6 = (bf16[528,128]{1,0:T(8,128)(2,1)S(1)}, bf16[528,128]{1,0:T(8,128)(2,1)S(1)}, u32[]{:S(2)}, u32[]{:S(2)}) collective-permute-start(bf16[528,128]{1,0:T(8,128)(2,1)S(1)} %get-tuple-element.38), channel_id=1, source_target_pairs={{0,12},{4,8},{8,4},{12,0},{16,28},{20,24},{24,20},{28,16},{1,13},{... | collective-permute-start | bytes 405512 | tf_op jit(solution)/shard_map/ppermute | solution.py:401
  9.4 14.8 %copy-start.4 = (bf16[2,128,512]{2,1,0:T(8,128)(2,1)S(1)}, bf16[2,128,512]{2,1,0:T(8,128)(2,1)}, u32[]{:S(2)}) copy-start(bf16[2,128,512]{2,1,0:T(8,128)(2,1)} %refs_4_.2) | copy-start | bytes 786436
  11.5 35.9 %copy-start.1 = (bf16[2,1024,128]{2,1,0:T(8,128)(2,1)S(1)}, bf16[2,1024,128]{2,1,0:T(8,128)(2,1)}, u32[]{:S(2)}) copy-start(bf16[2,1024,128]{2,1,0:T(8,128)(2,1)} %refs_3_.1) | copy-start | bytes 1572868
  11.5 9.3 %collective-permute-start = (bf16[528,128]{1,0:T(8,128)(2,1)S(1)}, bf16[528,128]{1,0:T(8,128)(2,1)S(1)}, u32[]{:S(2)}, u32[]{:S(2)}) collective-permute-start(bf16[528,128]{1,0:T(8,128)(2,1)S(1)} %get-tuple-element.30), channel_id=1, source_target_pairs={{0,4},{4,0},{8,12},{12,8},{16,20},{20,16},{24,28},{28,24},{1,5},{5... | collective-permute-start | bytes 405512 | tf_op jit(solution)/shard_map/ppermute | solution.py:401
  13.5 9.0 %collective-permute-start.1 = (bf16[528,128]{1,0:T(8,128)(2,1)S(1)}, bf16[528,128]{1,0:T(8,128)(2,1)S(1)}, u32[]{:S(2)}, u32[]{:S(2)}) collective-permute-start(bf16[528,128]{1,0:T(8,128)(2,1)S(1)} %get-tuple-element.31), channel_id=1, source_target_pairs={{0,8},{4,12},{8,0},{12,4},{16,24},{20,28},{24,16},{28,20},{1,9},{5... | collective-permute-start | bytes 405512 | tf_op jit(solution)/shard_map/ppermute | solution.py:401
  15.0 9.2 %collective-permute-start.2 = (bf16[528,128]{1,0:T(8,128)(2,1)S(1)}, bf16[528,128]{1,0:T(8,128)(2,1)S(1)}, u32[]{:S(2)}, u32[]{:S(2)}) collective-permute-start(bf16[528,128]{1,0:T(8,128)(2,1)S(1)} %get-tuple-element.32), channel_id=1, source_target_pairs={{0,12},{4,8},{8,4},{12,0},{16,28},{20,24},{24,20},{28,16},{1,13},{... | collective-permute-start | bytes 405512 | tf_op jit(solution)/shard_map/ppermute | solution.py:401
  16.6 12.8 %collective-permute-start.7 = (bf16[128,512]{1,0:T(8,128)(2,1)S(1)}, bf16[128,512]{1,0:T(8,128)(2,1)S(1)}, u32[]{:S(2)}, u32[]{:S(2)}) collective-permute-start(bf16[128,512]{1,0:T(8,128)(2,1)S(1)} %get-tuple-element.39), channel_id=1, source_target_pairs={{0,16},{4,20},{8,24},{12,28},{16,0},{20,4},{24,8},{28,12},{1,17},{... | collective-permute-start | bytes 393224 | tf_op jit(solution)/shard_map/ppermute | solution.py:401
  19.5 12.2 %collective-permute-start.8 = (bf16[128,512]{1,0:T(8,128)(2,1)S(1)}, bf16[128,512]{1,0:T(8,128)(2,1)S(1)}, u32[]{:S(2)}, u32[]{:S(2)}) collective-permute-start(bf16[128,512]{1,0:T(8,128)(2,1)S(1)} %get-tuple-element.40), channel_id=1, source_target_pairs={{0,20},{4,16},{8,28},{12,24},{16,4},{20,0},{24,12},{28,8},{1,21},{... | collective-permute-start | bytes 393224 | tf_op jit(solution)/shard_map/ppermute | solution.py:401
  24.5 23.6 %copy-start = (bf16[2,1024,128]{2,1,0:T(8,128)(2,1)S(1)}, bf16[2,1024,128]{2,1,0:T(8,128)(2,1)}, u32[]{:S(2)}) copy-start(bf16[2,1024,128]{2,1,0:T(8,128)(2,1)} %tiles.1) | copy-start | bytes 1572868
  24.5 7.2 %collective-permute-start.3 = (bf16[128,512]{1,0:T(8,128)(2,1)S(1)}, bf16[128,512]{1,0:T(8,128)(2,1)S(1)}, u32[]{:S(2)}, u32[]{:S(2)}) collective-permute-start(bf16[128,512]{1,0:T(8,128)(2,1)S(1)} %get-tuple-element.34), channel_id=1, source_target_pairs={{0,4},{4,0},{8,12},{12,8},{16,20},{20,16},{24,28},{28,24},{1,5},{5... | collective-permute-start | bytes 393224 | tf_op jit(solution)/shard_map/ppermute | solution.py:401
  31.7 11.3 %collective-permute-start.9 = (bf16[128,512]{1,0:T(8,128)(2,1)S(1)}, bf16[128,512]{1,0:T(8,128)(2,1)S(1)}, u32[]{:S(2)}, u32[]{:S(2)}) collective-permute-start(bf16[128,512]{1,0:T(8,128)(2,1)S(1)} %get-tuple-element.41.refs_0_), channel_id=1, source_target_pairs={{0,16},{4,20},{16,24},{20,28},{1,17},{5,21},{17,25},{21,29},{2,18}... | collective-permute-start | bytes 393224 | tf_op jit(solution)/shard_map/ppermute | solution.py:446
  34.4 13.0 %collective-permute-start.15 = (bf16[2,1024,128]{2,1,0:T(8,128)(2,1)S(1)}, bf16[2,1024,128]{2,1,0:T(8,128)(2,1)S(1)}, u32[]{:S(2)}, u32[]{:S(2)}) collective-permute-start(bf16[2,1024,128]{2,1,0:T(8,128)(2,1)S(1)} %get-tuple-element.43), channel_id=1, source_target_pairs={{0,4},{4,0},{8,12},{12,8},{16,20},{20,16},{24,28},{28,24},{1,5},{5... | collective-permute-start | bytes 1572872 | tf_op jit(solution)/shard_map/ppermute | solution.py:401
  35.4 11.0 %collective-permute-start.13 = (bf16[128,512]{1,0:T(8,128)(2,1)S(1)}, bf16[128,512]{1,0:T(8,128)(2,1)S(1)}, u32[]{:S(2)}, u32[]{:S(2)}) collective-permute-start(bf16[128,512]{1,0:T(8,128)(2,1)S(1)} %get-tuple-element.41.refs_0_), channel_id=1, source_target_pairs={{0,8},{4,12},{8,24},{12,28},{1,9},{5,13},{9,25},{13,29},{2,10},{6,... | collective-permute-start | bytes 393224 | tf_op jit(solution)/shard_map/ppermute | solution.py:446
  36.6 9.7 %collective-permute-start.14 = (bf16[128,512]{1,0:T(8,128)(2,1)S(1)}, bf16[128,512]{1,0:T(8,128)(2,1)S(1)}, u32[]{:S(2)}, u32[]{:S(2)}) collective-permute-start(bf16[128,512]{1,0:T(8,128)(2,1)S(1)} %get-tuple-element.42.refs_1_), channel_id=1, source_target_pairs={{0,8},{4,12},{8,24},{12,28},{1,9},{5,13},{9,25},{13,29},{2,10},{6,... | collective-permute-start | bytes 393224 | tf_op jit(solution)/shard_map/ppermute | solution.py:446
  41.7 3.9 %collective-permute-start.11 = (bf16[128,512]{1,0:T(8,128)(2,1)S(1)}, bf16[128,512]{1,0:T(8,128)(2,1)S(1)}, u32[]{:S(2)}, u32[]{:S(2)}) collective-permute-start(bf16[128,512]{1,0:T(8,128)(2,1)S(1)} %get-tuple-element.42.refs_1_), channel_id=1, source_target_pairs={{0,16},{4,20},{16,24},{20,28},{1,17},{5,21},{17,25},{21,29},{2,18}... | collective-permute-start | bytes 393224 | tf_op jit(solution)/shard_map/ppermute | solution.py:446
  43.0 5.0 %collective-permute-start.10 = (bf16[128,512]{1,0:T(8,128)(2,1)S(1)}, bf16[128,512]{1,0:T(8,128)(2,1)S(1)}, u32[]{:S(2)}, u32[]{:S(2)}) collective-permute-start(bf16[128,512]{1,0:T(8,128)(2,1)S(1)} %broadcast_select_fusion.1), channel_id=1, source_target_pairs={{8,16},{12,20},{16,24},{20,28},{9,17},{13,21},{17,25},{21,29},{10,... | collective-permute-start | bytes 393224 | tf_op jit(solution)/shard_map/ppermute | solution.py:446
  45.6 2.4 %collective-permute-start.12 = (bf16[128,512]{1,0:T(8,128)(2,1)S(1)}, bf16[128,512]{1,0:T(8,128)(2,1)S(1)}, u32[]{:S(2)}, u32[]{:S(2)}) collective-permute-start(bf16[128,512]{1,0:T(8,128)(2,1)S(1)} %broadcast_select_fusion), channel_id=1, source_target_pairs={{8,16},{12,20},{16,24},{20,28},{9,17},{13,21},{17,25},{21,29},{10,... | collective-permute-start | bytes 393224 | tf_op jit(solution)/shard_map/ppermute | solution.py:446
  48.0 23.8 %copy-start.3 = (bf16[2,256,512]{2,1,0:T(8,128)(2,1)S(1)}, bf16[2,256,512]{2,1,0:T(8,128)(2,1)}, u32[]{:S(2)}) copy-start(bf16[2,256,512]{2,1,0:T(8,128)(2,1)} %rhs.1) | copy-start | bytes 1572868
  48.7 30.1 %copy-start.2 = (bf16[2,1024,256]{2,1,0:T(8,128)(2,1)S(1)}, bf16[2,1024,256]{2,1,0:T(8,128)(2,1)}, u32[]{:S(2)}) copy-start(bf16[2,1024,256]{2,1,0:T(8,128)(2,1)} %refs_2_.1) | copy-start | bytes 3145732
  48.7 2.0 %collective-permute-start.17 = (bf16[2,256,512]{2,1,0:T(8,128)(2,1)S(1)}, bf16[2,256,512]{2,1,0:T(8,128)(2,1)S(1)}, u32[]{:S(2)}, u32[]{:S(2)}) collective-permute-start(bf16[2,256,512]{2,1,0:T(8,128)(2,1)S(1)} %get-tuple-element.46), channel_id=1, source_target_pairs={{0,1},{1,0},{2,3},{3,2},{4,5},{5,4},{6,7},{7,6},{8,9},{9,8},{10,11... | collective-permute-start | bytes 1572872 | tf_op jit(solution)/shard_map/ppermute | solution.py:404
  51.1 9.8 %collective-permute-start.18 = (bf16[512,128]{1,0:T(8,128)(2,1)S(1)}, bf16[512,128]{1,0:T(8,128)(2,1)S(1)}, u32[]{:S(2)}, u32[]{:S(2)}) collective-permute-start(bf16[512,128]{1,0:T(8,128)(2,1)S(1)} %get-tuple-element.48), channel_id=1, source_target_pairs={{0,8},{4,12},{8,0},{12,4},{16,24},{20,28},{24,16},{28,20},{1,9},{5... | collective-permute-start | bytes 393224 | tf_op jit(solution)/shard_map/ppermute | solution.py:401
  57.1 13.1 %collective-permute-start.19 = (bf16[512,128]{1,0:T(8,128)(2,1)S(1)}, bf16[512,128]{1,0:T(8,128)(2,1)S(1)}, u32[]{:S(2)}, u32[]{:S(2)}) collective-permute-start(bf16[512,128]{1,0:T(8,128)(2,1)S(1)} %get-tuple-element.49), channel_id=1, source_target_pairs={{0,16},{4,20},{8,24},{12,28},{16,0},{20,4},{24,8},{28,12},{1,17},{... | collective-permute-start | bytes 393224 | tf_op jit(solution)/shard_map/ppermute | solution.py:401
  60.3 10.0 %collective-permute-start.20 = (bf16[512,128]{1,0:T(8,128)(2,1)S(1)}, bf16[512,128]{1,0:T(8,128)(2,1)S(1)}, u32[]{:S(2)}, u32[]{:S(2)}) collective-permute-start(bf16[512,128]{1,0:T(8,128)(2,1)S(1)} %get-tuple-element.50), channel_id=1, source_target_pairs={{0,24},{4,28},{8,16},{12,20},{16,8},{20,12},{24,0},{28,4},{1,25},{... | collective-permute-start | bytes 393224 | tf_op jit(solution)/shard_map/ppermute | solution.py:401
  70.3 5.9 %collective-permute-start.21 = (bf16[512,128]{1,0:T(8,128)(2,1)S(1)}, bf16[512,128]{1,0:T(8,128)(2,1)S(1)}, u32[]{:S(2)}, u32[]{:S(2)}) collective-permute-start(bf16[512,128]{1,0:T(8,128)(2,1)S(1)} %shard_map.118.refs_0_), channel_id=1, source_target_pairs={{0,2},{1,3},{2,0},{3,1},{4,6},{5,7},{6,4},{7,5},{8,10},{9,11},{10,... | collective-permute-start | bytes 393224 | tf_op jit(solution)/shard_map/ppermute | solution.py:404
  71.9 4.3 %collective-permute-start.22 = (bf16[256,128]{1,0:T(8,128)(2,1)S(1)}, bf16[256,128]{1,0:T(8,128)(2,1)S(1)}, u32[]{:S(2)}, u32[]{:S(2)}) collective-permute-start(bf16[256,128]{1,0:T(8,128)(2,1)S(1)} %shard_map.119.refs_2_), channel_id=1, source_target_pairs={{0,2},{1,3},{2,0},{3,1},{4,6},{5,7},{6,4},{7,5},{8,10},{9,11},{10,... | collective-permute-start | bytes 196616 | tf_op jit(solution)/shard_map/ppermute | solution.py:404
  76.3 2.5 %collective-permute-start.23 = (bf16[512,128]{1,0:T(8,128)(2,1)S(1)}, bf16[512,128]{1,0:T(8,128)(2,1)S(1)}, u32[]{:S(2)}, u32[]{:S(2)}) collective-permute-start(bf16[512,128]{1,0:T(8,128)(2,1)S(1)} %shard_map.120.refs_0_), channel_id=1, source_target_pairs={{0,1},{1,0},{2,3},{3,2},{4,5},{5,4},{6,7},{7,6},{8,9},{9,8},{10,11... | collective-permute-start | bytes 393224 | tf_op jit(solution)/shard_map/ppermute | solution.py:404
  76.3 15.0 %collective-permute-start.16 = (bf16[128,512]{1,0:T(8,128)(2,1)S(1)}, bf16[128,512]{1,0:T(8,128)(2,1)S(1)}, u32[]{:S(2)}, u32[]{:S(2)}) collective-permute-start(bf16[128,512]{1,0:T(8,128)(2,1)S(1)} %get-tuple-element.45.other), channel_id=1, source_target_pairs={{0,4},{4,0},{8,12},{12,8},{16,20},{20,16},{24,28},{28,24},{1,5},{5... | collective-permute-start | bytes 393224 | tf_op jit(solution)/shard_map/ppermute | solution.py:401
  79.1 6.1 %collective-permute-start.29 = (bf16[256,128]{1,0:T(8,128)(2,1)S(1)}, bf16[256,128]{1,0:T(8,128)(2,1)S(1)}, u32[]{:S(2)}, u32[]{:S(2)}) collective-permute-start(bf16[256,128]{1,0:T(8,128)(2,1)S(1)} %shard_map.121.refs_0_), channel_id=1, source_target_pairs={{0,24},{4,28},{8,16},{12,20},{16,8},{20,12},{24,0},{28,4},{1,25},{... | collective-permute-start | bytes 196616 | tf_op jit(solution)/shard_map/ppermute | solution.py:401
  81.7 7.7 %collective-permute-start.27 = (bf16[256,128]{1,0:T(8,128)(2,1)S(1)}, bf16[256,128]{1,0:T(8,128)(2,1)S(1)}, u32[]{:S(2)}, u32[]{:S(2)}) collective-permute-start(bf16[256,128]{1,0:T(8,128)(2,1)S(1)} %shard_map.121.refs_0_), channel_id=1, source_target_pairs={{0,16},{4,20},{8,24},{12,28},{16,0},{20,4},{24,8},{28,12},{1,17},{... | collective-permute-start | bytes 196616 | tf_op jit(solution)/shard_map/ppermute | solution.py:401
  83.5 7.1 %collective-permute-start.25 = (bf16[256,128]{1,0:T(8,128)(2,1)S(1)}, bf16[256,128]{1,0:T(8,128)(2,1)S(1)}, u32[]{:S(2)}, u32[]{:S(2)}) collective-permute-start(bf16[256,128]{1,0:T(8,128)(2,1)S(1)} %shard_map.121.refs_0_), channel_id=1, source_target_pairs={{0,8},{4,12},{8,0},{12,4},{16,24},{20,28},{24,16},{28,20},{1,9},{5... | collective-permute-start | bytes 196616 | tf_op jit(solution)/shard_map/ppermute | solution.py:401
  83.6 8.5 %collective-permute-start.24 = (bf16[256,128]{1,0:T(8,128)(2,1)S(1)}, bf16[256,128]{1,0:T(8,128)(2,1)S(1)}, u32[]{:S(2)}, u32[]{:S(2)}) collective-permute-start(bf16[256,128]{1,0:T(8,128)(2,1)S(1)} %shard_map.121.refs_0_), channel_id=1, source_target_pairs={{0,4},{4,0},{8,12},{12,8},{16,20},{20,16},{24,28},{28,24},{1,5},{5... | collective-permute-start | bytes 196616 | tf_op jit(solution)/shard_map/ppermute | solution.py:401
  85.2 6.9 %collective-permute-start.30 = (bf16[256,128]{1,0:T(8,128)(2,1)S(1)}, bf16[256,128]{1,0:T(8,128)(2,1)S(1)}, u32[]{:S(2)}, u32[]{:S(2)}) collective-permute-start(bf16[256,128]{1,0:T(8,128)(2,1)S(1)} %collective-permute-done.29.refs_6_), channel_id=1, source_target_pairs={{0,4},{4,0},{8,12},{12,8},{16,20},{20,16},{24,28},{28,24},{1,5},{5... | collective-permute-start | bytes 196616 | tf_op jit(solution)/shard_map/ppermute | solution.py:401
  89.3 5.0 %collective-permute-start.28 = (bf16[256,128]{1,0:T(8,128)(2,1)S(1)}, bf16[256,128]{1,0:T(8,128)(2,1)S(1)}, u32[]{:S(2)}, u32[]{:S(2)}) collective-permute-start(bf16[256,128]{1,0:T(8,128)(2,1)S(1)} %collective-permute-done.27.refs_4_), channel_id=1, source_target_pairs={{0,4},{4,0},{8,12},{12,8},{16,20},{20,16},{24,28},{28,24},{1,5},{5... | collective-permute-start | bytes 196616 | tf_op jit(solution)/shard_map/ppermute | solution.py:401
  90.6 4.4 %collective-permute-start.26 = (bf16[256,128]{1,0:T(8,128)(2,1)S(1)}, bf16[256,128]{1,0:T(8,128)(2,1)S(1)}, u32[]{:S(2)}, u32[]{:S(2)}) collective-permute-start(bf16[256,128]{1,0:T(8,128)(2,1)S(1)} %collective-permute-done.25.refs_2_), channel_id=1, source_target_pairs={{0,4},{4,0},{8,12},{12,8},{16,20},{20,16},{24,28},{28,24},{1,5},{5... | collective-permute-start | bytes 196616 | tf_op jit(solution)/shard_map/ppermute | solution.py:401
where the time goes:
time: 96.1 us; the launch traced here: 95.9 us
  starting transfers between devices  50.7 us (53%)
  waiting for transfers between devices  33.9 us (35%)
  Pallas kernels  8.97 us (9%)
  between operations  1.53 us (2%)
    ppermute x21, starting transfers between devices, row_xor(): return lax.ppermute(x, 'row', [(i, i ^ k) for i in range(n_row)])  36.8 us
    ppermute x21, waiting for transfers between devices, row_xor(): return lax.ppermute(x, 'row', [(i, i ^ k) for i in range(n_row)])  26.3 us
    ppermute x6, starting transfers between devices, move(): return lax.ppermute(block, 'row', pairs)  11.6 us
    pallas_call x11, Pallas kernels, call(): pl.pallas_call(body, out_shape=[jax.ShapeDtypeStruct(s, BF16) for s in sh...  8.14 us
    ppermute x4, waiting for transfers between devices, col_xor(): return lax.ppermute(x, 'col', [(i, i ^ k) for i in range(n_col)])  5.61 us
    ppermute x4, starting transfers between devices, col_xor(): return lax.ppermute(x, 'col', [(i, i ^ k) for i in range(n_col)])  2.3 us
  transfers between devices with their start and end apart: 31, of which 15 were waited for; matrix products, arithmetic and copies ran while one was open for 1% of the time, Pallas kernels for 4%

commit v1 on v0

--- a/solution.py
+++ b/solution.py
@@ -71,13 +71,13 @@
     step = min(256, depth // 2)
     count = depth // step
 
-    def body(inverse_hbm, rhs_hbm, tiles_hbm, slot, solved_hbm, solved, *rest):
+    def body(inverse_hbm, rhs_hbm, tiles_hbm, slot, solved, *rest):
         blocks = rest[:half]
         inverse, rhs, tiles, update, sems = rest[half:]
         row = lax.axis_index("row")
         base = (1 - row // half) * (depth // 2)
         spans = [slice(i * step, (i + 1) * step) for i in range(count)]
-        first, second, stored = [], [], []
+        first, second = [], []
         for i, span in enumerate(spans):
             left = slice(0, (i + 1) * step)
             first.append(fetch(rhs_hbm.at[span], rhs.at[span], sems.at[0, i]))
@@ -92,17 +92,14 @@
             first[2 * i + 1].wait()
             block = dot(inverse[span, : (i + 1) * step], rhs[: (i + 1) * step, :], 1)
             solved[span, :] = block.astype(BF16)
-            stored.append(fetch(solved.at[span], solved_hbm.at[span], sems.at[3, i]))
         for i in range(count // 2):
             second[i].wait()
             update[spans[i], :] = dot(tiles[spans[i], :], solved[...], 1).astype(BF16)
         write_blocks(blocks, update, slot, rows, row % half)
-        for copy in stored:
-            copy.wait()
 
     out = call(
         body,
-        [(depth, src)] * 2 + [(src // LANES * rows + MARK, LANES)] * half,
+        [(depth, src)] + [(src // LANES * rows + MARK, LANES)] * half,
         (*map(in_hbm, (leaf_inverse, leaf_rhs, leaf_tiles)), tile_lists),
         [HBM, HBM, HBM, SMEM],
         [
@@ -110,11 +107,10 @@
             pltpu.VMEM((depth, src), BF16),
             pltpu.VMEM((depth // 2, depth), BF16),
             pltpu.VMEM((depth // 2, src), BF16),
-            pltpu.SemaphoreType.DMA((4, count)),
+            pltpu.SemaphoreType.DMA((3, count)),
         ],
-        [HBM] + [VMEM] * (half + 1),
     )
-    return out[0], out[1], out[2:]
+    return out[0], out[1:]
 
 
 def near_stage(solved, leaf_tiles, tile_lists, mid_inverse_t, mid_tiles, n_row):
@@ -123,7 +119,7 @@
     half = n_row // 2
     rows = depth // n_row
 
-    def body(solved, tiles_hbm, slot, mid_inverse, mid_tile, swap, *rest):
+    def body(solved, tiles_hbm, slot, mid_inverse, mid_tile, solved_hbm, swap, *rest):
         blocks, (tiles, update, sems) = rest[:half], rest[half:]
         row = lax.axis_index("row")
         at = pl.ds(pl.multiple_of(row // half * (depth // 2), depth // 2), depth // 2)
@@ -131,6 +127,7 @@
             fetch(tiles_hbm.at[at], tiles, sems.at[0]),
             fetch(mid_inverse.at[1 - row % nb], swap.at[0], sems.at[1]),
             fetch(mid_tile.at[1 - row % nb], swap.at[1], sems.at[2]),
+            fetch(solved, solved_hbm, sems.at[3]),
         ]
         copies[0].wait()
         update[...] = dot(tiles[...], solved[...], 1).astype(BF16)
@@ -140,16 +137,17 @@
 
     out = call(
         body,
-        [(2, depth, own_rows)] + [(src // LANES * rows + MARK, LANES)] * half,
+        [(depth, src), (2, depth, own_rows)] + [(src // LANES * rows + MARK, LANES)] * half,
         (solved, in_hbm(leaf_tiles), tile_lists, *map(in_hbm, (mid_inverse_t, mid_tiles))),
         [VMEM, HBM, SMEM, HBM, HBM],
         [
             pltpu.VMEM((depth // 2, depth), BF16),
             pltpu.VMEM((depth // 2, src), BF16),
-            pltpu.SemaphoreType.DMA((3,)),
+            pltpu.SemaphoreType.DMA((4,)),
         ],
+        [HBM] + [VMEM] * (half + 1),
     )
-    return out[0], out[1:]
+    return out[0], out[1], out[2:]
 
 
 def slot_sums(blocks, nb, rows, chunk):
@@ -419,10 +417,10 @@
         src = leaf_rhs.shape[2]
         n_z = n_row // n_top
 
-        solved_leaf, solved, far = leaf_stage(
+        solved, far = leaf_stage(
             leaf_inverse[0], leaf_rhs[0], leaf_tiles[0], tile_lists, n_row
         )
-        swap, near = near_stage(
+        solved_leaf, swap, near = near_stage(
             solved, leaf_tiles[0], tile_lists, mid_inverse_t, mid_tiles, n_row
         )
 
@@ -446,7 +444,10 @@
             return lax.ppermute(block, "row", pairs)
 
         near_given = row_xor(other, 1)
-        start = resid_stage((near_mine, far_mine), (near_given, far_given))
+        start = (
+            *resid_stage((near_mine, far_mine)),
+            *resid_stage((near_given, far_given)),
+        )
         blocks, owners = [start], [lambda z: z]
         if n_z == 4:
             z = lax.axis_index("row") // nb

time: 96.1 us -> 93.8 us (0.976)
  waiting for transfers between devices: 33.9 us -> 28.5 us
  starting transfers between devices: 50.7 us -> 53.4 us
    ppermute x21, waiting for transfers between devices: 26.3 us -> 20.9 us  [row_xor(): return lax.ppermute(x, 'row', [(i, i ^ k) for i in range(n_row)])]
    ppermute x6, starting transfers between devices: 11.6 us -> 13.5 us  [move(): return lax.ppermute(block, 'row', pairs)]
    pallas_call x11 -> x12, Pallas kernels: 8.14 us -> 8.47 us  [call(): pl.pallas_call(body, out_shape=[jax.ShapeDtypeStruct(s, BF16) for s in sh...]
  transfers between devices with their start and end apart: 31 -> 31, of which waited for: 15 -> 13; matrix products, arithmetic and copies ran while one was open for 1% -> 1% of each run, Pallas kernels for 4% -> 4%
where the time goes in v1:
time: 93.8 us; the launch traced here: 93.6 us
  starting transfers between devices  53.4 us (57%)
  waiting for transfers between devices  28.5 us (30%)
  Pallas kernels  9.3 us (10%)
  between operations  1.57 us (2%)
    ppermute x21, starting transfers between devices, row_xor(): return lax.ppermute(x, 'row', [(i, i ^ k) for i in range(n_row)])  37.7 us
    ppermute x21, waiting for transfers between devices, row_xor(): return lax.ppermute(x, 'row', [(i, i ^ k) for i in range(n_row)])  20.9 us
    ppermute x6, starting transfers between devices, move(): return lax.ppermute(block, 'row', pairs)  13.5 us
    pallas_call x12, Pallas kernels, call(): pl.pallas_call(body, out_shape=[jax.ShapeDtypeStruct(s, BF16) for s in sh...  8.47 us
    ppermute x4, waiting for transfers between devices, col_xor(): return lax.ppermute(x, 'col', [(i, i ^ k) for i in range(n_col)])  5.73 us
    ppermute x4, starting transfers between devices, col_xor(): return lax.ppermute(x, 'col', [(i, i ^ k) for i in range(n_col)])  2.3 us
    ppermute x6, waiting for transfers between devices, move(): return lax.ppermute(block, 'row', pairs)  1.91 us
  transfers between devices with their start and end apart: 31, of which 13 were waited for; matrix products, arithmetic and copies ran while one was open for 1% of the time, Pallas kernels for 4%

profile of v1, /device:TPU:0, one launch (start us, length us, event | category | flops | bytes accessed | tf_op | source)
XLA Modules:
  0.0 93.6 jit_solution(14100911068595540254)
XLA Ops:
  1.3 3.4 %shard_map.112 = (bf16[1024,512]{1,0:T(8,128)(2,1)S(1)}, bf16[528,128]{1,0:T(8,128)(2,1)S(1)}, bf16[528,128]{1,0:T(8,128)(2,1)S(1)}, bf16[528,128]{1,0:T(8,128)(2,1)S(1)}, bf16[528,128]{1,0:T(8,128)(2,1)S(1)}) custom-call(bf16[1024,1024]{1,0:T(8,128)(2,1)} %bitcast.9, bf16[1024,512]{1,0:T(8,128)(2,1)} %bitcast.10, bf16[1024,1024]{1,0:T(8,128)(2,1)} %bitcast.7, ...), custom_call_target="tpu_custom_call" | custom-call | tf_op jit(solution)/shard_map/pallas_call | solution.py:40
  4.7 3.1 %collective-permute-start.3 = (bf16[528,128]{1,0:T(8,128)(2,1)S(1)}, bf16[528,128]{1,0:T(8,128)(2,1)S(1)}, u32[]{:S(2)}, u32[]{:S(2)}) collective-permute-start(bf16[528,128]{1,0:T(8,128)(2,1)S(1)} %get-tuple-element.33), channel_id=1, source_target_pairs={{0,4},{4,0},{8,12},{12,8},{16,20},{20,16},{24,28},{28,24},{1,5},{5... | collective-permute-start | bytes 405512 | tf_op jit(solution)/shard_map/ppermute | solution.py:399
  7.8 1.6 %collective-permute-start.4 = (bf16[528,128]{1,0:T(8,128)(2,1)S(1)}, bf16[528,128]{1,0:T(8,128)(2,1)S(1)}, u32[]{:S(2)}, u32[]{:S(2)}) collective-permute-start(bf16[528,128]{1,0:T(8,128)(2,1)S(1)} %get-tuple-element.34), channel_id=1, source_target_pairs={{0,8},{4,12},{8,0},{12,4},{16,24},{20,28},{24,16},{28,20},{1,9},{5... | collective-permute-start | bytes 405512 | tf_op jit(solution)/shard_map/ppermute | solution.py:399
  9.3 0.0 collective-permute-start.5
  9.3 2.5 %shard_map.113 = (bf16[1024,512]{1,0:T(8,128)(2,1)}, bf16[2,1024,128]{2,1,0:T(8,128)(2,1)S(1)}, bf16[528,128]{1,0:T(8,128)(2,1)S(1)}, bf16[528,128]{1,0:T(8,128)...) custom-call(bf16[1024,512]{1,0:T(8,128)(2,1)S(1)} %get-tuple-element.25.solved, ...), custom_call_target="tpu_custom_call" | custom-call | tf_op jit(solution)/shard_map/pallas_call | solution.py:40
  11.8 0.0 copy-start.1
  11.8 2.0 %collective-permute-start = (bf16[528,128]{1,0:T(8,128)(2,1)S(1)}, bf16[528,128]{1,0:T(8,128)(2,1)S(1)}, u32[]{:S(2)}, u32[]{:S(2)}) collective-permute-start(bf16[528,128]{1,0:T(8,128)(2,1)S(1)} %get-tuple-element.28), channel_id=1, source_target_pairs={{0,4},{4,0},{8,12},{12,8},{16,20},{20,16},{24,28},{28,24},{1,5},{5... | collective-permute-start | bytes 405512 | tf_op jit(solution)/shard_map/ppermute | solution.py:399
  13.8 1.6 %collective-permute-start.1 = (bf16[528,128]{1,0:T(8,128)(2,1)S(1)}, bf16[528,128]{1,0:T(8,128)(2,1)S(1)}, u32[]{:S(2)}, u32[]{:S(2)}) collective-permute-start(bf16[528,128]{1,0:T(8,128)(2,1)S(1)} %get-tuple-element.29), channel_id=1, source_target_pairs={{0,8},{4,12},{8,0},{12,4},{16,24},{20,28},{24,16},{28,20},{1,9},{5... | collective-permute-start | bytes 405512 | tf_op jit(solution)/shard_map/ppermute | solution.py:399
  15.4 0.0 collective-permute-done.3.refs_1_
  15.4 0.0 collective-permute-start.2
  15.4 0.7 collective-permute-done.5.refs_3_
  16.0 0.2 shard_map.114
  16.2 2.9 %collective-permute-start.6 = (bf16[128,512]{1,0:T(8,128)(2,1)S(1)}, bf16[128,512]{1,0:T(8,128)(2,1)S(1)}, u32[]{:S(2)}, u32[]{:S(2)}) collective-permute-start(bf16[128,512]{1,0:T(8,128)(2,1)S(1)} %get-tuple-element.36), channel_id=1, source_target_pairs={{0,16},{4,20},{8,24},{12,28},{16,0},{20,4},{24,8},{28,12},{1,17},{... | collective-permute-start | bytes 393224 | tf_op jit(solution)/shard_map/ppermute | solution.py:399
  19.1 1.3 %collective-permute-start.10 = (bf16[128,512]{1,0:T(8,128)(2,1)S(1)}, bf16[128,512]{1,0:T(8,128)(2,1)S(1)}, u32[]{:S(2)}, u32[]{:S(2)}) collective-permute-start(bf16[128,512]{1,0:T(8,128)(2,1)S(1)} %get-tuple-element.38), channel_id=1, source_target_pairs={{0,20},{4,16},{8,28},{12,24},{16,4},{20,0},{24,12},{28,8},{1,21},{... | collective-permute-start | bytes 393224 | tf_op jit(solution)/shard_map/ppermute | solution.py:399
  20.4 2.7 %collective-permute-done.1.refs_2_ = bf16[528,128]{1,0:T(8,128)(2,1)S(1)} collective-permute-done((bf16[528,128]{1,0:T(8,128)(2,1)S(1)}, bf16[528,128]{1,0:T(8,128)(2,1)S(1)}, u32[]{:S(2)}, u32[]{:S(2)}) %collective-permute-start.1) | collective-permute-done | bytes 135200 | tf_op jit(solution)/shard_map/ppermute | solution.py:399
  23.1 1.1 %collective-permute-done.2.refs_3_ = bf16[528,128]{1,0:T(8,128)(2,1)S(1)} collective-permute-done((bf16[528,128]{1,0:T(8,128)(2,1)S(1)}, bf16[528,128]{1,0:T(8,128)(2,1)S(1)}, u32[]{:S(2)}, u32[]{:S(2)}) %collective-permute-start.2) | collective-permute-done | bytes 135200 | tf_op jit(solution)/shard_map/ppermute | solution.py:399
  24.2 0.2 near_sum.1
  24.5 0.0 copy-start
  24.5 3.0 %collective-permute-start.9 = (bf16[128,512]{1,0:T(8,128)(2,1)S(1)}, bf16[128,512]{1,0:T(8,128)(2,1)S(1)}, u32[]{:S(2)}, u32[]{:S(2)}) collective-permute-start(bf16[128,512]{1,0:T(8,128)(2,1)S(1)} %get-tuple-element.37), channel_id=1, source_target_pairs={{0,4},{4,0},{8,12},{12,8},{16,20},{20,16},{24,28},{28,24},{1,5},{5... | collective-permute-start | bytes 393224 | tf_op jit(solution)/shard_map/ppermute | solution.py:399
  27.5 0.0 collective-permute-done.6.refs_1_
  27.5 2.7 %collective-permute-start.7 = (bf16[128,512]{1,0:T(8,128)(2,1)S(1)}, bf16[128,512]{1,0:T(8,128)(2,1)S(1)}, u32[]{:S(2)}, u32[]{:S(2)}) collective-permute-start(bf16[128,512]{1,0:T(8,128)(2,1)S(1)} %shard_map.115.refs_0_), channel_id=1, source_target_pairs={{0,16},{4,20},{16,24},{20,28},{1,17},{5,21},{17,25},{21,29},{2,18}... | collective-permute-start | bytes 393224 | tf_op jit(solution)/shard_map/ppermute | solution.py:444
  30.2 2.0 %collective-permute-start.15 = (bf16[2,1024,128]{2,1,0:T(8,128)(2,1)S(1)}, bf16[2,1024,128]{2,1,0:T(8,128)(2,1)S(1)}, u32[]{:S(2)}, u32[]{:S(2)}) collective-permute-start(bf16[2,1024,128]{2,1,0:T(8,128)(2,1)S(1)} %get-tuple-element.39), channel_id=1, source_target_pairs={{0,4},{4,0},{8,12},{12,8},{16,20},{20,16},{24,28},{28,24},{1,5},{5... | collective-permute-start | bytes 1572872 | tf_op jit(solution)/shard_map/ppermute | solution.py:399
  32.2 2.1 %collective-permute-start.13 = (bf16[128,512]{1,0:T(8,128)(2,1)S(1)}, bf16[128,512]{1,0:T(8,128)(2,1)S(1)}, u32[]{:S(2)}, u32[]{:S(2)}) collective-permute-start(bf16[128,512]{1,0:T(8,128)(2,1)S(1)} %shard_map.115.refs_0_), channel_id=1, source_target_pairs={{0,8},{4,12},{8,24},{12,28},{1,9},{5,13},{9,25},{13,29},{2,10},{6,... | collective-permute-start | bytes 393224 | tf_op jit(solution)/shard_map/ppermute | solution.py:444
  34.4 6.0 %collective-permute-start.14 = (bf16[128,512]{1,0:T(8,128)(2,1)S(1)}, bf16[128,512]{1,0:T(8,128)(2,1)S(1)}, u32[]{:S(2)}, u32[]{:S(2)}) collective-permute-start(bf16[128,512]{1,0:T(8,128)(2,1)S(1)} %shard_map.116.refs_1_), channel_id=1, source_target_pairs={{0,8},{4,12},{8,24},{12,28},{1,9},{5,13},{9,25},{13,29},{2,10},{6,... | collective-permute-start | bytes 393224 | tf_op jit(solution)/shard_map/ppermute | solution.py:444
  40.4 1.3 %collective-permute-start.11 = (bf16[128,512]{1,0:T(8,128)(2,1)S(1)}, bf16[128,512]{1,0:T(8,128)(2,1)S(1)}, u32[]{:S(2)}, u32[]{:S(2)}) collective-permute-start(bf16[128,512]{1,0:T(8,128)(2,1)S(1)} %shard_map.116.refs_1_), channel_id=1, source_target_pairs={{0,16},{4,20},{16,24},{20,28},{1,17},{5,21},{17,25},{21,29},{2,18}... | collective-permute-start | bytes 393224 | tf_op jit(solution)/shard_map/ppermute | solution.py:444
  41.7 0.0 collective-permute-done.7.refs_2_
  41.8 0.7 collective-permute-start.8
  42.4 1.9 %collective-permute-done.11.refs_3_ = bf16[128,512]{1,0:T(8,128)(2,1)S(1)} collective-permute-done((bf16[128,512]{1,0:T(8,128)(2,1)S(1)}, bf16[128,512]{1,0:T(8,128)(2,1)S(1)}, u32[]{:S(2)}, u32[]{:S(2)}) %collective-permute-start.11) | collective-permute-done | bytes 131104 | tf_op jit(solution)/shard_map/ppermute | solution.py:444
  44.3 0.7 collective-permute-start.12
  45.0 0.0 collective-permute-done.15.refs_7_.refs_5_.swap
  45.1 0.6 early.1.refs_2_
  45.7 0.0 copy-start.3
  45.7 0.0 collective-permute-done.12.refs_1_
  45.7 0.6 shard_map.117
  46.3 0.0 copy-start.2
  46.3 0.1 collective-permute-start.17
  46.4 1.9 %collective-permute-done.17.far = bf16[2,256,512]{2,1,0:T(8,128)(2,1)S(1)} collective-permute-done((bf16[2,256,512]{2,1,0:T(8,128)(2,1)S(1)}, bf16[2,256,512]{2,1,0:T(8,128)(2,1)S(1)}, u32[]{:S(2)}, u32[]{:S(2)}) %collective-permute-start.17) | collective-permute-done | bytes 524320 | tf_op jit(solution)/shard_map/ppermute | solution.py:402
  48.3 0.4 shard_map.118
  48.7 7.1 %collective-permute-start.18 = (bf16[512,128]{1,0:T(8,128)(2,1)S(1)}, bf16[512,128]{1,0:T(8,128)(2,1)S(1)}, u32[]{:S(2)}, u32[]{:S(2)}) collective-permute-start(bf16[512,128]{1,0:T(8,128)(2,1)S(1)} %get-tuple-element.44), channel_id=1, source_target_pairs={{0,8},{4,12},{8,0},{12,4},{16,24},{20,28},{24,16},{28,20},{1,9},{5... | collective-permute-start | bytes 393224 | tf_op jit(solution)/shard_map/ppermute | solution.py:399
  55.8 3.5 %collective-permute-start.19 = (bf16[512,128]{1,0:T(8,128)(2,1)S(1)}, bf16[512,128]{1,0:T(8,128)(2,1)S(1)}, u32[]{:S(2)}, u32[]{:S(2)}) collective-permute-start(bf16[512,128]{1,0:T(8,128)(2,1)S(1)} %get-tuple-element.45), channel_id=1, source_target_pairs={{0,16},{4,20},{8,24},{12,28},{16,0},{20,4},{24,8},{28,12},{1,17},{... | collective-permute-start | bytes 393224 | tf_op jit(solution)/shard_map/ppermute | solution.py:399
  59.3 0.3 collective-permute-done.18.refs_1_
  59.6 9.7 %collective-permute-done.19.refs_2_ = bf16[512,128]{1,0:T(8,128)(2,1)S(1)} collective-permute-done((bf16[512,128]{1,0:T(8,128)(2,1)S(1)}, bf16[512,128]{1,0:T(8,128)(2,1)S(1)}, u32[]{:S(2)}, u32[]{:S(2)}) %collective-permute-start.19) | collective-permute-done | bytes 131104 | tf_op jit(solution)/shard_map/ppermute | solution.py:399
  69.3 0.1 shard_map.119.refs_0_
  69.4 1.5 %collective-permute-start.21 = (bf16[512,128]{1,0:T(8,128)(2,1)S(1)}, bf16[512,128]{1,0:T(8,128)(2,1)S(1)}, u32[]{:S(2)}, u32[]{:S(2)}) collective-permute-start(bf16[512,128]{1,0:T(8,128)(2,1)S(1)} %shard_map.119.refs_0_), channel_id=1, source_target_pairs={{0,2},{1,3},{2,0},{3,1},{4,6},{5,7},{6,4},{7,5},{8,10},{9,11},{10,... | collective-permute-start | bytes 393224 | tf_op jit(solution)/shard_map/ppermute | solution.py:402
  70.8 0.7 collective-permute-start.22
  71.5 3.6 %collective-permute-done.22.refs_3_ = bf16[256,128]{1,0:T(8,128)(2,1)S(1)} collective-permute-done((bf16[256,128]{1,0:T(8,128)(2,1)S(1)}, bf16[256,128]{1,0:T(8,128)(2,1)S(1)}, u32[]{:S(2)}, u32[]{:S(2)}) %collective-permute-start.22) | collective-permute-done | bytes 65568 | tf_op jit(solution)/shard_map/ppermute | solution.py:402
  75.2 0.1 shard_map.121.refs_0_
  75.3 0.1 collective-permute-start.23
  75.3 1.1 %collective-permute-start.16 = (bf16[128,512]{1,0:T(8,128)(2,1)S(1)}, bf16[128,512]{1,0:T(8,128)(2,1)S(1)}, u32[]{:S(2)}, u32[]{:S(2)}) collective-permute-start(bf16[128,512]{1,0:T(8,128)(2,1)S(1)} %get-tuple-element.41.other), channel_id=1, source_target_pairs={{0,4},{4,0},{8,12},{12,8},{16,20},{20,16},{24,28},{28,24},{1,5},{5... | collective-permute-start | bytes 393224 | tf_op jit(solution)/shard_map/ppermute | solution.py:399
  76.5 0.2 collective-permute-done.23.refs_1_
  76.7 0.4 shard_map.122.refs_0_
  77.0 2.9 %collective-permute-start.29 = (bf16[256,128]{1,0:T(8,128)(2,1)S(1)}, bf16[256,128]{1,0:T(8,128)(2,1)S(1)}, u32[]{:S(2)}, u32[]{:S(2)}) collective-permute-start(bf16[256,128]{1,0:T(8,128)(2,1)S(1)} %shard_map.122.refs_0_), channel_id=1, source_target_pairs={{0,24},{4,28},{8,16},{12,20},{16,8},{20,12},{24,0},{28,4},{1,25},{... | collective-permute-start | bytes 196616 | tf_op jit(solution)/shard_map/ppermute | solution.py:399
  79.9 1.5 %collective-permute-start.27 = (bf16[256,128]{1,0:T(8,128)(2,1)S(1)}, bf16[256,128]{1,0:T(8,128)(2,1)S(1)}, u32[]{:S(2)}, u32[]{:S(2)}) collective-permute-start(bf16[256,128]{1,0:T(8,128)(2,1)S(1)} %shard_map.122.refs_0_), channel_id=1, source_target_pairs={{0,16},{4,20},{8,24},{12,28},{16,0},{20,4},{24,8},{28,12},{1,17},{... | collective-permute-start | bytes 196616 | tf_op jit(solution)/shard_map/ppermute | solution.py:399
  81.4 0.0 collective-permute-start.25
  81.5 1.1 %collective-permute-start.24 = (bf16[256,128]{1,0:T(8,128)(2,1)S(1)}, bf16[256,128]{1,0:T(8,128)(2,1)S(1)}, u32[]{:S(2)}, u32[]{:S(2)}) collective-permute-start(bf16[256,128]{1,0:T(8,128)(2,1)S(1)} %shard_map.122.refs_0_), channel_id=1, source_target_pairs={{0,4},{4,0},{8,12},{12,8},{16,20},{20,16},{24,28},{28,24},{1,5},{5... | collective-permute-start | bytes 196616 | tf_op jit(solution)/shard_map/ppermute | solution.py:399
  82.5 0.6 collective-permute-done.29.refs_6_
  83.2 1.1 %collective-permute-start.30 = (bf16[256,128]{1,0:T(8,128)(2,1)S(1)}, bf16[256,128]{1,0:T(8,128)(2,1)S(1)}, u32[]{:S(2)}, u32[]{:S(2)}) collective-permute-start(bf16[256,128]{1,0:T(8,128)(2,1)S(1)} %collective-permute-done.29.refs_6_), channel_id=1, source_target_pairs={{0,4},{4,0},{8,12},{12,8},{16,20},{20,16},{24,28},{28,24},{1,5},{5... | collective-permute-start | bytes 196616 | tf_op jit(solution)/shard_map/ppermute | solution.py:399
  84.2 3.0 %collective-permute-done.27.refs_4_ = bf16[256,128]{1,0:T(8,128)(2,1)S(1)} collective-permute-done((bf16[256,128]{1,0:T(8,128)(2,1)S(1)}, bf16[256,128]{1,0:T(8,128)(2,1)S(1)}, u32[]{:S(2)}, u32[]{:S(2)}) %collective-permute-start.27) | collective-permute-done | bytes 65568 | tf_op jit(solution)/shard_map/ppermute | solution.py:399
  87.3 1.1 %collective-permute-start.28 = (bf16[256,128]{1,0:T(8,128)(2,1)S(1)}, bf16[256,128]{1,0:T(8,128)(2,1)S(1)}, u32[]{:S(2)}, u32[]{:S(2)}) collective-permute-start(bf16[256,128]{1,0:T(8,128)(2,1)S(1)} %collective-permute-done.27.refs_4_), channel_id=1, source_target_pairs={{0,4},{4,0},{8,12},{12,8},{16,20},{20,16},{24,28},{28,24},{1,5},{5... | collective-permute-start | bytes 196616 | tf_op jit(solution)/shard_map/ppermute | solution.py:399
  88.3 1.0 %collective-permute-start.26 = (bf16[256,128]{1,0:T(8,128)(2,1)S(1)}, bf16[256,128]{1,0:T(8,128)(2,1)S(1)}, u32[]{:S(2)}, u32[]{:S(2)}) collective-permute-start(bf16[256,128]{1,0:T(8,128)(2,1)S(1)} %collective-permute-done.25.refs_2_), channel_id=1, source_target_pairs={{0,4},{4,0},{8,12},{12,8},{16,20},{20,16},{24,28},{28,24},{1,5},{5... | collective-permute-start | bytes 196616 | tf_op jit(solution)/shard_map/ppermute | solution.py:399
  89.3 0.7 maximum_select_fusion
  90.0 2.0 %collective-permute-done.28.refs_5_ = bf16[256,128]{1,0:T(8,128)(2,1)S(1)} collective-permute-done((bf16[256,128]{1,0:T(8,128)(2,1)S(1)}, bf16[256,128]{1,0:T(8,128)(2,1)S(1)}, u32[]{:S(2)}, u32[]{:S(2)}) %collective-permute-start.28) | collective-permute-done | bytes 65568 | tf_op jit(solution)/shard_map/ppermute | solution.py:399
  92.0 0.7 collective-permute-done.26.refs_3_
  92.7 0.8 shard_map.123
  (25 shorter events, 0.2 us)
Async XLA Ops:
  4.7 10.7 %collective-permute-start.3 = (bf16[528,128]{1,0:T(8,128)(2,1)S(1)}, bf16[528,128]{1,0:T(8,128)(2,1)S(1)}, u32[]{:S(2)}, u32[]{:S(2)}) collective-permute-start(bf16[528,128]{1,0:T(8,128)(2,1)S(1)} %get-tuple-element.33), channel_id=1, source_target_pairs={{0,4},{4,0},{8,12},{12,8},{16,20},{20,16},{24,28},{28,24},{1,5},{5... | collective-permute-start | bytes 405512 | tf_op jit(solution)/shard_map/ppermute | solution.py:399
  7.8 7.6 %collective-permute-start.4 = (bf16[528,128]{1,0:T(8,128)(2,1)S(1)}, bf16[528,128]{1,0:T(8,128)(2,1)S(1)}, u32[]{:S(2)}, u32[]{:S(2)}) collective-permute-start(bf16[528,128]{1,0:T(8,128)(2,1)S(1)} %get-tuple-element.34), channel_id=1, source_target_pairs={{0,8},{4,12},{8,0},{12,4},{16,24},{20,28},{24,16},{28,20},{1,9},{5... | collective-permute-start | bytes 405512 | tf_op jit(solution)/shard_map/ppermute | solution.py:399
  9.3 6.7 %collective-permute-start.5 = (bf16[528,128]{1,0:T(8,128)(2,1)S(1)}, bf16[528,128]{1,0:T(8,128)(2,1)S(1)}, u32[]{:S(2)}, u32[]{:S(2)}) collective-permute-start(bf16[528,128]{1,0:T(8,128)(2,1)S(1)} %get-tuple-element.35), channel_id=1, source_target_pairs={{0,12},{4,8},{8,4},{12,0},{16,28},{20,24},{24,20},{28,16},{1,13},{... | collective-permute-start | bytes 405512 | tf_op jit(solution)/shard_map/ppermute | solution.py:399
  9.3 14.9 %copy-start.4 = (bf16[2,128,512]{2,1,0:T(8,128)(2,1)S(1)}, bf16[2,128,512]{2,1,0:T(8,128)(2,1)}, u32[]{:S(2)}) copy-start(bf16[2,128,512]{2,1,0:T(8,128)(2,1)} %refs_4_.2) | copy-start | bytes 786436
  11.8 33.3 %copy-start.1 = (bf16[2,1024,128]{2,1,0:T(8,128)(2,1)S(1)}, bf16[2,1024,128]{2,1,0:T(8,128)(2,1)}, u32[]{:S(2)}) copy-start(bf16[2,1024,128]{2,1,0:T(8,128)(2,1)} %refs_3_.1) | copy-start | bytes 1572868
  11.8 8.6 %collective-permute-start = (bf16[528,128]{1,0:T(8,128)(2,1)S(1)}, bf16[528,128]{1,0:T(8,128)(2,1)S(1)}, u32[]{:S(2)}, u32[]{:S(2)}) collective-permute-start(bf16[528,128]{1,0:T(8,128)(2,1)S(1)} %get-tuple-element.28), channel_id=1, source_target_pairs={{0,4},{4,0},{8,12},{12,8},{16,20},{20,16},{24,28},{28,24},{1,5},{5... | collective-permute-start | bytes 405512 | tf_op jit(solution)/shard_map/ppermute | solution.py:399
  13.8 9.3 %collective-permute-start.1 = (bf16[528,128]{1,0:T(8,128)(2,1)S(1)}, bf16[528,128]{1,0:T(8,128)(2,1)S(1)}, u32[]{:S(2)}, u32[]{:S(2)}) collective-permute-start(bf16[528,128]{1,0:T(8,128)(2,1)S(1)} %get-tuple-element.29), channel_id=1, source_target_pairs={{0,8},{4,12},{8,0},{12,4},{16,24},{20,28},{24,16},{28,20},{1,9},{5... | collective-permute-start | bytes 405512 | tf_op jit(solution)/shard_map/ppermute | solution.py:399
  15.4 8.9 %collective-permute-start.2 = (bf16[528,128]{1,0:T(8,128)(2,1)S(1)}, bf16[528,128]{1,0:T(8,128)(2,1)S(1)}, u32[]{:S(2)}, u32[]{:S(2)}) collective-permute-start(bf16[528,128]{1,0:T(8,128)(2,1)S(1)} %get-tuple-element.30), channel_id=1, source_target_pairs={{0,12},{4,8},{8,4},{12,0},{16,28},{20,24},{24,20},{28,16},{1,13},{... | collective-permute-start | bytes 405512 | tf_op jit(solution)/shard_map/ppermute | solution.py:399
  16.2 11.2 %collective-permute-start.6 = (bf16[128,512]{1,0:T(8,128)(2,1)S(1)}, bf16[128,512]{1,0:T(8,128)(2,1)S(1)}, u32[]{:S(2)}, u32[]{:S(2)}) collective-permute-start(bf16[128,512]{1,0:T(8,128)(2,1)S(1)} %get-tuple-element.36), channel_id=1, source_target_pairs={{0,16},{4,20},{8,24},{12,28},{16,0},{20,4},{24,8},{28,12},{1,17},{... | collective-permute-start | bytes 393224 | tf_op jit(solution)/shard_map/ppermute | solution.py:399
  19.1 15.3 %collective-permute-start.10 = (bf16[128,512]{1,0:T(8,128)(2,1)S(1)}, bf16[128,512]{1,0:T(8,128)(2,1)S(1)}, u32[]{:S(2)}, u32[]{:S(2)}) collective-permute-start(bf16[128,512]{1,0:T(8,128)(2,1)S(1)} %get-tuple-element.38), channel_id=1, source_target_pairs={{0,20},{4,16},{8,28},{12,24},{16,4},{20,0},{24,12},{28,8},{1,21},{... | collective-permute-start | bytes 393224 | tf_op jit(solution)/shard_map/ppermute | solution.py:399
  24.5 21.2 %copy-start = (bf16[2,1024,128]{2,1,0:T(8,128)(2,1)S(1)}, bf16[2,1024,128]{2,1,0:T(8,128)(2,1)}, u32[]{:S(2)}) copy-start(bf16[2,1024,128]{2,1,0:T(8,128)(2,1)} %tiles.1) | copy-start | bytes 1572868
  24.5 9.9 %collective-permute-start.9 = (bf16[128,512]{1,0:T(8,128)(2,1)S(1)}, bf16[128,512]{1,0:T(8,128)(2,1)S(1)}, u32[]{:S(2)}, u32[]{:S(2)}) collective-permute-start(bf16[128,512]{1,0:T(8,128)(2,1)S(1)} %get-tuple-element.37), channel_id=1, source_target_pairs={{0,4},{4,0},{8,12},{12,8},{16,20},{20,16},{24,28},{28,24},{1,5},{5... | collective-permute-start | bytes 393224 | tf_op jit(solution)/shard_map/ppermute | solution.py:399
  27.5 14.2 %collective-permute-start.7 = (bf16[128,512]{1,0:T(8,128)(2,1)S(1)}, bf16[128,512]{1,0:T(8,128)(2,1)S(1)}, u32[]{:S(2)}, u32[]{:S(2)}) collective-permute-start(bf16[128,512]{1,0:T(8,128)(2,1)S(1)} %shard_map.115.refs_0_), channel_id=1, source_target_pairs={{0,16},{4,20},{16,24},{20,28},{1,17},{5,21},{17,25},{21,29},{2,18}... | collective-permute-start | bytes 393224 | tf_op jit(solution)/shard_map/ppermute | solution.py:444
  30.2 14.8 %collective-permute-start.15 = (bf16[2,1024,128]{2,1,0:T(8,128)(2,1)S(1)}, bf16[2,1024,128]{2,1,0:T(8,128)(2,1)S(1)}, u32[]{:S(2)}, u32[]{:S(2)}) collective-permute-start(bf16[2,1024,128]{2,1,0:T(8,128)(2,1)S(1)} %get-tuple-element.39), channel_id=1, source_target_pairs={{0,4},{4,0},{8,12},{12,8},{16,20},{20,16},{24,28},{28,24},{1,5},{5... | collective-permute-start | bytes 1572872 | tf_op jit(solution)/shard_map/ppermute | solution.py:399
  32.2 12.8 %collective-permute-start.13 = (bf16[128,512]{1,0:T(8,128)(2,1)S(1)}, bf16[128,512]{1,0:T(8,128)(2,1)S(1)}, u32[]{:S(2)}, u32[]{:S(2)}) collective-permute-start(bf16[128,512]{1,0:T(8,128)(2,1)S(1)} %shard_map.115.refs_0_), channel_id=1, source_target_pairs={{0,8},{4,12},{8,24},{12,28},{1,9},{5,13},{9,25},{13,29},{2,10},{6,... | collective-permute-start | bytes 393224 | tf_op jit(solution)/shard_map/ppermute | solution.py:444
  34.4 10.6 %collective-permute-start.14 = (bf16[128,512]{1,0:T(8,128)(2,1)S(1)}, bf16[128,512]{1,0:T(8,128)(2,1)S(1)}, u32[]{:S(2)}, u32[]{:S(2)}) collective-permute-start(bf16[128,512]{1,0:T(8,128)(2,1)S(1)} %shard_map.116.refs_1_), channel_id=1, source_target_pairs={{0,8},{4,12},{8,24},{12,28},{1,9},{5,13},{9,25},{13,29},{2,10},{6,... | collective-permute-start | bytes 393224 | tf_op jit(solution)/shard_map/ppermute | solution.py:444
  40.4 3.9 %collective-permute-start.11 = (bf16[128,512]{1,0:T(8,128)(2,1)S(1)}, bf16[128,512]{1,0:T(8,128)(2,1)S(1)}, u32[]{:S(2)}, u32[]{:S(2)}) collective-permute-start(bf16[128,512]{1,0:T(8,128)(2,1)S(1)} %shard_map.116.refs_1_), channel_id=1, source_target_pairs={{0,16},{4,20},{16,24},{20,28},{1,17},{5,21},{17,25},{21,29},{2,18}... | collective-permute-start | bytes 393224 | tf_op jit(solution)/shard_map/ppermute | solution.py:444
  41.8 3.9 %collective-permute-start.8 = (bf16[128,512]{1,0:T(8,128)(2,1)S(1)}, bf16[128,512]{1,0:T(8,128)(2,1)S(1)}, u32[]{:S(2)}, u32[]{:S(2)}) collective-permute-start(bf16[128,512]{1,0:T(8,128)(2,1)S(1)} %broadcast_select_fusion.1), channel_id=1, source_target_pairs={{8,16},{12,20},{16,24},{20,28},{9,17},{13,21},{17,25},{21,29},{10,... | collective-permute-start | bytes 393224 | tf_op jit(solution)/shard_map/ppermute | solution.py:444
  44.3 1.4 %collective-permute-start.12 = (bf16[128,512]{1,0:T(8,128)(2,1)S(1)}, bf16[128,512]{1,0:T(8,128)(2,1)S(1)}, u32[]{:S(2)}, u32[]{:S(2)}) collective-permute-start(bf16[128,512]{1,0:T(8,128)(2,1)S(1)} %broadcast_select_fusion), channel_id=1, source_target_pairs={{8,16},{12,20},{16,24},{20,28},{9,17},{13,21},{17,25},{21,29},{10,... | collective-permute-start | bytes 393224 | tf_op jit(solution)/shard_map/ppermute | solution.py:444
  45.7 25.2 %copy-start.3 = (bf16[2,256,512]{2,1,0:T(8,128)(2,1)S(1)}, bf16[2,256,512]{2,1,0:T(8,128)(2,1)}, u32[]{:S(2)}) copy-start(bf16[2,256,512]{2,1,0:T(8,128)(2,1)} %rhs.1) | copy-start | bytes 1572868
  46.3 30.3 %copy-start.2 = (bf16[2,1024,256]{2,1,0:T(8,128)(2,1)S(1)}, bf16[2,1024,256]{2,1,0:T(8,128)(2,1)}, u32[]{:S(2)}) copy-start(bf16[2,1024,256]{2,1,0:T(8,128)(2,1)} %refs_2_.1) | copy-start | bytes 3145732
  46.3 2.0 %collective-permute-start.17 = (bf16[2,256,512]{2,1,0:T(8,128)(2,1)S(1)}, bf16[2,256,512]{2,1,0:T(8,128)(2,1)S(1)}, u32[]{:S(2)}, u32[]{:S(2)}) collective-permute-start(bf16[2,256,512]{2,1,0:T(8,128)(2,1)S(1)} %get-tuple-element.42), channel_id=1, source_target_pairs={{0,1},{1,0},{2,3},{3,2},{4,5},{5,4},{6,7},{7,6},{8,9},{9,8},{10,11... | collective-permute-start | bytes 1572872 | tf_op jit(solution)/shard_map/ppermute | solution.py:402
  48.7 10.9 %collective-permute-start.18 = (bf16[512,128]{1,0:T(8,128)(2,1)S(1)}, bf16[512,128]{1,0:T(8,128)(2,1)S(1)}, u32[]{:S(2)}, u32[]{:S(2)}) collective-permute-start(bf16[512,128]{1,0:T(8,128)(2,1)S(1)} %get-tuple-element.44), channel_id=1, source_target_pairs={{0,8},{4,12},{8,0},{12,4},{16,24},{20,28},{24,16},{28,20},{1,9},{5... | collective-permute-start | bytes 393224 | tf_op jit(solution)/shard_map/ppermute | solution.py:399
  55.8 13.5 %collective-permute-start.19 = (bf16[512,128]{1,0:T(8,128)(2,1)S(1)}, bf16[512,128]{1,0:T(8,128)(2,1)S(1)}, u32[]{:S(2)}, u32[]{:S(2)}) collective-permute-start(bf16[512,128]{1,0:T(8,128)(2,1)S(1)} %get-tuple-element.45), channel_id=1, source_target_pairs={{0,16},{4,20},{8,24},{12,28},{16,0},{20,4},{24,8},{28,12},{1,17},{... | collective-permute-start | bytes 393224 | tf_op jit(solution)/shard_map/ppermute | solution.py:399
  59.3 10.0 %collective-permute-start.20 = (bf16[512,128]{1,0:T(8,128)(2,1)S(1)}, bf16[512,128]{1,0:T(8,128)(2,1)S(1)}, u32[]{:S(2)}, u32[]{:S(2)}) collective-permute-start(bf16[512,128]{1,0:T(8,128)(2,1)S(1)} %get-tuple-element.46), channel_id=1, source_target_pairs={{0,24},{4,28},{8,16},{12,20},{16,8},{20,12},{24,0},{28,4},{1,25},{... | collective-permute-start | bytes 393224 | tf_op jit(solution)/shard_map/ppermute | solution.py:399
  69.4 5.8 %collective-permute-start.21 = (bf16[512,128]{1,0:T(8,128)(2,1)S(1)}, bf16[512,128]{1,0:T(8,128)(2,1)S(1)}, u32[]{:S(2)}, u32[]{:S(2)}) collective-permute-start(bf16[512,128]{1,0:T(8,128)(2,1)S(1)} %shard_map.119.refs_0_), channel_id=1, source_target_pairs={{0,2},{1,3},{2,0},{3,1},{4,6},{5,7},{6,4},{7,5},{8,10},{9,11},{10,... | collective-permute-start | bytes 393224 | tf_op jit(solution)/shard_map/ppermute | solution.py:402
  70.8 4.3 %collective-permute-start.22 = (bf16[256,128]{1,0:T(8,128)(2,1)S(1)}, bf16[256,128]{1,0:T(8,128)(2,1)S(1)}, u32[]{:S(2)}, u32[]{:S(2)}) collective-permute-start(bf16[256,128]{1,0:T(8,128)(2,1)S(1)} %shard_map.120.refs_2_), channel_id=1, source_target_pairs={{0,2},{1,3},{2,0},{3,1},{4,6},{5,7},{6,4},{7,5},{8,10},{9,11},{10,... | collective-permute-start | bytes 196616 | tf_op jit(solution)/shard_map/ppermute | solution.py:402
  75.3 1.4 %collective-permute-start.23 = (bf16[512,128]{1,0:T(8,128)(2,1)S(1)}, bf16[512,128]{1,0:T(8,128)(2,1)S(1)}, u32[]{:S(2)}, u32[]{:S(2)}) collective-permute-start(bf16[512,128]{1,0:T(8,128)(2,1)S(1)} %shard_map.121.refs_0_), channel_id=1, source_target_pairs={{0,1},{1,0},{2,3},{3,2},{4,5},{5,4},{6,7},{7,6},{8,9},{9,8},{10,11... | collective-permute-start | bytes 393224 | tf_op jit(solution)/shard_map/ppermute | solution.py:402
  75.3 14.0 %collective-permute-start.16 = (bf16[128,512]{1,0:T(8,128)(2,1)S(1)}, bf16[128,512]{1,0:T(8,128)(2,1)S(1)}, u32[]{:S(2)}, u32[]{:S(2)}) collective-permute-start(bf16[128,512]{1,0:T(8,128)(2,1)S(1)} %get-tuple-element.41.other), channel_id=1, source_target_pairs={{0,4},{4,0},{8,12},{12,8},{16,20},{20,16},{24,28},{28,24},{1,5},{5... | collective-permute-start | bytes 393224 | tf_op jit(solution)/shard_map/ppermute | solution.py:399
  77.0 6.1 %collective-permute-start.29 = (bf16[256,128]{1,0:T(8,128)(2,1)S(1)}, bf16[256,128]{1,0:T(8,128)(2,1)S(1)}, u32[]{:S(2)}, u32[]{:S(2)}) collective-permute-start(bf16[256,128]{1,0:T(8,128)(2,1)S(1)} %shard_map.122.refs_0_), channel_id=1, source_target_pairs={{0,24},{4,28},{8,16},{12,20},{16,8},{20,12},{24,0},{28,4},{1,25},{... | collective-permute-start | bytes 196616 | tf_op jit(solution)/shard_map/ppermute | solution.py:399
  79.9 7.4 %collective-permute-start.27 = (bf16[256,128]{1,0:T(8,128)(2,1)S(1)}, bf16[256,128]{1,0:T(8,128)(2,1)S(1)}, u32[]{:S(2)}, u32[]{:S(2)}) collective-permute-start(bf16[256,128]{1,0:T(8,128)(2,1)S(1)} %shard_map.122.refs_0_), channel_id=1, source_target_pairs={{0,16},{4,20},{8,24},{12,28},{16,0},{20,4},{24,8},{28,12},{1,17},{... | collective-permute-start | bytes 196616 | tf_op jit(solution)/shard_map/ppermute | solution.py:399
  81.4 6.9 %collective-permute-start.25 = (bf16[256,128]{1,0:T(8,128)(2,1)S(1)}, bf16[256,128]{1,0:T(8,128)(2,1)S(1)}, u32[]{:S(2)}, u32[]{:S(2)}) collective-permute-start(bf16[256,128]{1,0:T(8,128)(2,1)S(1)} %shard_map.122.refs_0_), channel_id=1, source_target_pairs={{0,8},{4,12},{8,0},{12,4},{16,24},{20,28},{24,16},{28,20},{1,9},{5... | collective-permute-start | bytes 196616 | tf_op jit(solution)/shard_map/ppermute | solution.py:399
  81.5 8.5 %collective-permute-start.24 = (bf16[256,128]{1,0:T(8,128)(2,1)S(1)}, bf16[256,128]{1,0:T(8,128)(2,1)S(1)}, u32[]{:S(2)}, u32[]{:S(2)}) collective-permute-start(bf16[256,128]{1,0:T(8,128)(2,1)S(1)} %shard_map.122.refs_0_), channel_id=1, source_target_pairs={{0,4},{4,0},{8,12},{12,8},{16,20},{20,16},{24,28},{28,24},{1,5},{5... | collective-permute-start | bytes 196616 | tf_op jit(solution)/shard_map/ppermute | solution.py:399
  83.2 6.9 %collective-permute-start.30 = (bf16[256,128]{1,0:T(8,128)(2,1)S(1)}, bf16[256,128]{1,0:T(8,128)(2,1)S(1)}, u32[]{:S(2)}, u32[]{:S(2)}) collective-permute-start(bf16[256,128]{1,0:T(8,128)(2,1)S(1)} %collective-permute-done.29.refs_6_), channel_id=1, source_target_pairs={{0,4},{4,0},{8,12},{12,8},{16,20},{20,16},{24,28},{28,24},{1,5},{5... | collective-permute-start | bytes 196616 | tf_op jit(solution)/shard_map/ppermute | solution.py:399
  87.3 4.8 %collective-permute-start.28 = (bf16[256,128]{1,0:T(8,128)(2,1)S(1)}, bf16[256,128]{1,0:T(8,128)(2,1)S(1)}, u32[]{:S(2)}, u32[]{:S(2)}) collective-permute-start(bf16[256,128]{1,0:T(8,128)(2,1)S(1)} %collective-permute-done.27.refs_4_), channel_id=1, source_target_pairs={{0,4},{4,0},{8,12},{12,8},{16,20},{20,16},{24,28},{28,24},{1,5},{5... | collective-permute-start | bytes 196616 | tf_op jit(solution)/shard_map/ppermute | solution.py:399
  88.3 4.4 %collective-permute-start.26 = (bf16[256,128]{1,0:T(8,128)(2,1)S(1)}, bf16[256,128]{1,0:T(8,128)(2,1)S(1)}, u32[]{:S(2)}, u32[]{:S(2)}) collective-permute-start(bf16[256,128]{1,0:T(8,128)(2,1)S(1)} %collective-permute-done.25.refs_2_), channel_id=1, source_target_pairs={{0,4},{4,0},{8,12},{12,8},{16,20},{20,16},{24,28},{28,24},{1,5},{5... | collective-permute-start | bytes 196616 | tf_op jit(solution)/shard_map/ppermute | solution.py:399
